TPU v7x, 128 devices: a whole 4x4x4 slice. The times are simulated.
128 devices in a mesh: grp: 8 (over z, core), tp: 16 (over x, y).
Axes of the slice: x: 4, y: 4, z: 4, core: 2. Of those that a mesh axis runs over, the one named last changes fastest.
Arguments:
- tokens: bfloat16 [4096, 4096], P('grp', 'tp'), may hold values from -6 to 6
- token_tenant: int32 [4096], P('grp'), may hold values from 0 to 63, as said below
- tenant_storage_slot: int32 [64], replicated, may hold values from 0 to 63, as said below
- gate_matrix: bfloat16 [4096, 14336], P(None, 'tp'), may hold values from -0.09375 to 0.09375
- up_matrix: bfloat16 [4096, 14336], P(None, 'tp'), may hold values from -0.09375 to 0.09375
- down_matrix: bfloat16 [14336, 4096], P('tp'), may hold values from -0.046875 to 0.046875
- adapter_gate_up_inputs: bfloat16 [64, 4096, 128], P('grp', 'tp'), may hold values from -0.09375 to 0.09375
- adapter_gate_up_outputs: bfloat16 [64, 128, 14336], P('grp', None, 'tp'), may hold values from -0.75 to 0.75
- adapter_down_inputs: bfloat16 [64, 14336, 64], P('grp', 'tp'), may hold values from -0.046875 to 0.046875
- adapter_down_outputs: bfloat16 [64, 64, 4096], P('grp', None, 'tp'), may hold values from -0.75 to 0.75
Outputs:
- mixed: bfloat16 [4096, 4096], P('grp', 'tp')
Inputs may be any that keep to these rules, and one draw needn't show every extreme that they name: `token_tenant`: within each aligned block of 512 tokens, at most 128 tokens have tenants whose slot lies in one storage block of 8 slots; one storage block, chosen from the seed, receives exactly 128 tokens from every such block. `tenant_storage_slot`: A permutation of the tenants.
All inputs are finite; a program needn't handle non-finite values.
Results may differ from a plain program's by a relative error of at most 0.017.
Values may be sent and summed in bfloat16 or wider, within the bound.
No kernel may reach another device: no remote copies, remote signals or barrier semaphores. Data moves between devices by JAX's collectives and lax.ppermute only.
A program may use at most 128 MiB of HBM per device.

v0:
```python
import jax
import jax.numpy as jnp
from jax import lax
from jax.sharding import PartitionSpec as P


def spread_onehot(onehot, vec):
    wide = onehot[:, :, None] * vec[:, None, :]
    return wide.reshape(vec.shape[0], -1)


def body(
    tokens,
    token_tenant,
    tenant_storage_slot,
    gate_matrix,
    up_matrix,
    down_matrix,
    adapter_gate_up_inputs,
    adapter_gate_up_outputs,
    adapter_down_inputs,
    adapter_down_outputs,
):
    groups = lax.axis_size("grp")
    rows = tokens.shape[0]
    block_slots = adapter_gate_up_inputs.shape[0]
    adapter_width = adapter_gate_up_inputs.shape[2] // 2
    hidden_share = gate_matrix.shape[1]
    width_share = tokens.shape[1]
    capacity = 2 * rows // groups
    table = jnp.arange(tenant_storage_slot.shape[0], dtype=jnp.int32)
    match = token_tenant[:, None] == table[None, :]
    slot = jnp.sum(jnp.where(match, tenant_storage_slot[None, :], 0), 1)
    server = slot // block_slots
    local = slot - server * block_slots
    picks = (server[:, None] == jnp.arange(groups, dtype=jnp.int32)[None, :]).astype(jnp.int32)
    place = jnp.sum(picks * (jnp.cumsum(picks, 0) - 1), 1)

    def pack(values, fill):
        buffer = jnp.full((groups, capacity) + values.shape[1:], fill, values.dtype)
        return buffer.at[server, place].set(values)

    sent_rows = pack(tokens, 0)
    sent_local = pack(local.astype(jnp.bfloat16), -1)
    got_rows, got_local = (
        lax.all_to_all(sent_rows, "grp", split_axis=0, concat_axis=0, tiled=True),
        lax.all_to_all(sent_local, "grp", split_axis=0, concat_axis=0, tiled=True),
    )
    rows_flattened = got_rows.reshape(groups * capacity, width_share)
    owner = got_local.reshape(-1).astype(jnp.float32)
    onehot = (owner[:, None] == jnp.arange(block_slots, dtype=jnp.float32)[None, :]).astype(
        jnp.bfloat16
    )
    onehot_wide = onehot.astype(jnp.float32)[:, :, None]
    part = jnp.einsum(
        "ny,eyq->neq", rows_flattened, adapter_gate_up_inputs, preferred_element_type=jnp.float32
    )
    part = jnp.sum(part * onehot_wide, 1)
    ranks = lax.psum(part, "tp").astype(jnp.bfloat16)
    gate_output_factor = adapter_gate_up_outputs[:, :adapter_width, :].reshape(
        block_slots * adapter_width, hidden_share
    )
    up_output_factor = adapter_gate_up_outputs[:, adapter_width:, :].reshape(
        block_slots * adapter_width, hidden_share
    )
    delta_gate = jnp.dot(
        spread_onehot(onehot, ranks[:, :adapter_width]),
        gate_output_factor,
        preferred_element_type=jnp.float32,
    ).astype(jnp.bfloat16)
    delta_up = jnp.dot(
        spread_onehot(onehot, ranks[:, adapter_width:]),
        up_output_factor,
        preferred_element_type=jnp.float32,
    ).astype(jnp.bfloat16)
    back_gate, back_up = (
        lax.all_to_all(
            delta_gate.reshape(groups, capacity, hidden_share),
            "grp",
            split_axis=0,
            concat_axis=0,
            tiled=True,
        ),
        lax.all_to_all(
            delta_up.reshape(groups, capacity, hidden_share),
            "grp",
            split_axis=0,
            concat_axis=0,
            tiled=True,
        ),
    )
    piece = lax.all_gather(tokens, "tp", axis=1, tiled=True)
    base_gate = jnp.dot(piece, gate_matrix, preferred_element_type=jnp.float32)
    base_up = jnp.dot(piece, up_matrix, preferred_element_type=jnp.float32)
    gate = base_gate + back_gate[server, place].astype(jnp.float32)
    up = base_up + back_up[server, place].astype(jnp.float32)
    hidden = (jax.nn.silu(gate) * up).astype(jnp.bfloat16)
    sent_hidden = pack(hidden, 0)
    got_hidden = lax.all_to_all(sent_hidden, "grp", split_axis=0, concat_axis=0, tiled=True)
    hidden_flattened = got_hidden.reshape(groups * capacity, hidden_share)
    down_part = jnp.einsum(
        "us,ysc->uyc", hidden_flattened, adapter_down_inputs, preferred_element_type=jnp.float32
    )
    down_part = jnp.sum(down_part * onehot_wide, 1)
    down_ranks = lax.psum(down_part.astype(jnp.bfloat16), "tp")
    down_output_factor = adapter_down_outputs.reshape(block_slots * adapter_width, width_share)
    delta_down = jnp.dot(
        spread_onehot(onehot, down_ranks), down_output_factor, preferred_element_type=jnp.float32
    ).astype(jnp.bfloat16)
    back_down = lax.all_to_all(
        delta_down.reshape(groups, capacity, width_share),
        "grp",
        split_axis=0,
        concat_axis=0,
        tiled=True,
    )
    returned = back_down[server, place].astype(jnp.float32)
    partial_value = jnp.dot(hidden, down_matrix, preferred_element_type=jnp.float32)
    result = (
        lax.psum_scatter(
            partial_value.astype(jnp.bfloat16), "tp", scatter_dimension=1, tiled=True
        ).astype(jnp.float32)
        + returned
    )
    return result.astype(jnp.bfloat16)


def solution(mesh):
    return jax.shard_map(
        body,
        mesh=mesh,
        in_specs=(
            P("grp", "tp"),
            P("grp"),
            P(),
            P(None, "tp"),
            P(None, "tp"),
            P("tp", None),
            P("grp", "tp", None),
            P("grp", None, "tp"),
            P("grp", "tp", None),
            P("grp", None, "tp"),
        ),
        out_specs=P("grp", "tp"),
        check_vma=False,
    )
```

profile of v0, /device:TPU:0, one launch (start us, length us, event | category | flops | bytes accessed | tf_op | source)
XLA Modules:
  0.0 527.4 jit_solution(13378956549153246454)
XLA Ops:
  6.5 0.7 all-gather.2.cloned.1.call-update
  7.3 0.8 select_reduce_fusion
  8.1 1.1 reduce-window.6
  9.6 22.6 %scatter_fusion = bf16[8,128]{1,0:T(8,128)(2,1)S(1)} fusion(bf16[8,128]{1,0:T(8,128)(2,1)S(1)} %broadcast_in_dim.18, s32[512]{0:T(512)S(1)} %bitcast.60, bf16[512]{0:T(512)(128)(2,1)S(1)} %get-tuple-element.5), kind=kCustom, calls=%fused_computation.3 | custom fusion | bytes 7168 | tf_op jit(solution)/shard_map/scatter | solution.py:41
  32.8 5.4 %all-to-all-start = ((bf16[8,1,128]{2,1,0:T(2,128)(2,1)}), bf16[8,1,128]{2,1,0:T(2,128)(2,1)S(1)}, u32[]{:S(2)}, u32[]{:S(2)}) async-start(bf16[8,1,128]{2,1,0:T(2,128)(2,1)} %copy.16), calls=%async_computation | async-start | bytes 8192 | tf_op jit(solution)/shard_map/all_to_all | solution.py:47
  38.3 0.8 broadcast_in_dim.21
  39.1 58.0 %scatter_fusion.1 = bf16[8,128,256]{2,1,0:T(8,128)(2,1)} fusion(bf16[8,128,256]{2,1,0:T(8,128)(2,1)} %broadcast_in_dim.21, s32[512]{0:T(512)S(1)} %bitcast.61, bf16[512,256]{1,0:T(8,128)(2,1)S(1)} %copy-done.1), kind=kCustom, calls=%fused_computation.4 | custom fusion | bytes 790528 | tf_op jit(solution)/shard_map/scatter | solution.py:41
  97.1 5.0 all-to-all-start.1
  102.1 10.3 %all-to-all-done.1 = bf16[8,128,256]{2,1,0:T(8,128)(2,1)S(1)} async-done(((bf16[8,128,256]{2,1,0:T(8,128)(2,1)}), bf16[8,128,256]{2,1,0:T(8,128)(2,1)S(1)}, u32[]{:S(2)}, u32[]{:S(2)}) %all-to-all-start.1) | async-done | bytes 524320 | tf_op jit(solution)/shard_map/all_to_all | solution.py:46
  112.4 1.8 multiply_reduce_fusion
  114.2 80.2 %all-reduce.4 = bf16[1024,128]{1,0:T(8,128)(2,1)S(1)} all-reduce(f32[1024,128]{1,0:T(8,128)S(1)} %multiply_reduce_fusion), channel_id=1, replica_groups=mesh['grp'=8,'tp'=16] {'tp'}, use_global_device_ids=true, to_apply=%region_7.8 | all-reduce | flops 131072 | bytes 786432 | tf_op jit(solution)/shard_map/psum | solution.py:59
  194.6 3.7 bitcast_convert_fusion.1
  198.4 3.6 all-to-all-start.2
  202.1 3.8 bitcast_convert_fusion
  205.9 20.4 %all-to-all-done.2 = bf16[8,128,896]{2,1,0:T(8,128)(2,1)S(1)} async-done(((bf16[8,128,896]{2,1,0:T(8,128)(2,1)}), bf16[8,128,896]{2,1,0:T(8,128)(2,1)S(1)}, u32[]{:S(2)}, u32[]{:S(2)}) %all-to-all-start.2) | async-done | bytes 1835040 | tf_op jit(solution)/shard_map/all_to_all | solution.py:77
  226.3 4.3 all-to-all-start.3
  230.8 7.7 %gather_fusion = bf16[512,896]{1,0:T(8,128)(2,1)} fusion(bf16[8,128,896]{2,1,0:T(8,128)(2,1)S(1)} %all-to-all-done.2, s32[512]{0:T(512)S(1)} %bitcast.63), kind=kCustom, calls=%fused_computation | custom fusion | bytes 1839104 | tf_op jit(solution)/shard_map/gather | solution.py:95
  238.5 16.5 %all-to-all-done.3 = bf16[8,128,896]{2,1,0:T(8,128)(2,1)} async-done(((bf16[8,128,896]{2,1,0:T(8,128)(2,1)}), bf16[8,128,896]{2,1,0:T(8,128)(2,1)}, u32[]{:S(2)}, u32[]{:S(2)}) %all-to-all-start.3) | async-done | bytes 1835040 | tf_op jit(solution)/shard_map/all_to_all | solution.py:84
  255.0 7.9 %gather_fusion.1 = bf16[512,896]{1,0:T(8,128)(2,1)S(1)} fusion(bf16[8,128,896]{2,1,0:T(8,128)(2,1)} %all-to-all-done.3, s32[512]{0:T(512)S(1)} %bitcast.64), kind=kCustom, calls=%fused_computation.1 | custom fusion | bytes 1839104 | tf_op jit(solution)/shard_map/gather | solution.py:96
  262.9 9.9 %fusion.24 = f32[512,896]{1,0:T(8,128)S(1)} fusion(bf16[512,4096]{1,0:T(8,128)(2,1)} %all-gather.2.cloned.1.call-done, bf16[4096,896]{1,0:T(8,128)(2,1)} %param.13), kind=kOutput, calls=%fused_computation.65 | convolution fusion | flops 3758096384 | bytes 13369344 | tf_op jit(solution)/shard_map/dot_general | solution.py:93
  272.8 8.8 %multiply_convert_fusion = bf16[512,896]{1,0:T(8,128)(2,1)} fusion(bf16[512,896]{1,0:T(8,128)(2,1)S(1)} %gather_fusion.1, f32[512,896]{1,0:T(8,128)S(1)} %fusion.24, bf16[512,896]{1,0:T(8,128)(2,1)S(1)} %copy-done.2, bf16[512,4096]{1,0:T(8,128)(2,1)S(1)} %copy-done.4, bf16[4096,896]{1,0:T(8,128)(2,1)} %param.14), kind=kOutput, calls=%fused_computation.11 | convolution fusion | flops 3762683904 | bytes 16121856 | tf_op jit(solution)/shard_map/dot_general | solution.py:94
  281.9 48.8 %scatter_fusion.2 = bf16[8,128,896]{2,1,0:T(8,128)(2,1)S(1)} fusion(bf16[8,128,896]{2,1,0:T(8,128)(2,1)S(1)} %broadcast_in_dim.22, s32[512]{0:T(512)S(1)} %bitcast.62, bf16[512,896]{1,0:T(8,128)(2,1)} %multiply_convert_fusion), kind=kCustom, calls=%fused_computation.5 | custom fusion | bytes 2756608 | tf_op jit(solution)/shard_map/scatter | solution.py:41
  330.7 26.8 %all_to_all.34 = bf16[8,128,896]{2,1,0:T(8,128)(2,1)S(1)} all-to-all(bf16[8,128,896]{2,1,0:T(8,128)(2,1)S(1)} %scatter_fusion.2), channel_id=1, replica_groups=mesh['grp'=8,'tp'=16] {'grp'}, dimensions={0} | all-to-all | bytes 3670016 | tf_op jit(solution)/shard_map/all_to_all | solution.py:99
  357.5 1.3 fusion.25
  358.8 0.9 multiply_reduce_fusion.1
  360.0 9.3 %convolution_convert_fusion = bf16[512,4096]{1,0:T(8,128)(2,1)} fusion(bf16[512,896]{1,0:T(8,128)(2,1)S(1)} %copy-done.3, bf16[896,4096]{1,0:T(8,128)(2,1)} %param.15), kind=kOutput, calls=%fused_computation.6 | convolution fusion | flops 3760193536 | bytes 12451840 | tf_op jit(solution)/shard_map/dot_general | solution.py:118
  369.3 68.7 %all-reduce.3.cloned.1.call-done = bf16[1024,64]{0,1:T(8,128)(2,1)} async-done(((bf16[1024,64]{0,1:T(8,128)(2,1)}), bf16[1024,64]{0,1:T(8,128)(2,1)}) %all-reduce.3.cloned.1.call-update) | async-done | bytes 131088 | tf_op jit(solution)/shard_map/psum | solution.py:105
  438.0 1.4 fusion
  439.4 14.6 %all_to_all.35 = bf16[8,128,256]{2,1,0:T(8,128)(2,1)S(1)} all-to-all(bf16[8,128,256]{2,1,0:T(8,128)(2,1)S(1)} %bitcast.71), channel_id=1, replica_groups=mesh['grp'=8,'tp'=16] {'grp'}, dimensions={0} | all-to-all | bytes 1048576 | tf_op jit(solution)/shard_map/all_to_all | solution.py:110
  454.0 3.2 gather_fusion.2
  457.2 62.0 %reduce-scatter.2.cloned.1.call-done = bf16[512,256]{1,0:T(8,128)(2,1)} async-done(((bf16[512,4096]{1,0:T(8,128)(2,1)}), bf16[512,256]{1,0:T(8,128)(2,1)}) %reduce-scatter.2.cloned.1.call-update) | async-done | bytes 262160 | tf_op jit(solution)/shard_map/reduce_scatter | solution.py:120
  519.1 1.7 add_convert_fusion
  (37 shorter events, 2.2 us)
Async XLA Ops:
  6.5 351.0 %copy-start = (bf16[8,896,64]{1,2,0:T(8,128)(2,1)S(1)}, bf16[8,896,64]{1,2,0:T(8,128)(2,1)}, u32[]{:S(2)}) copy-start(bf16[8,896,64]{1,2,0:T(8,128)(2,1)} %param.18) | copy-start | bytes 2752516
  6.5 32.6 %copy-start.1 = (bf16[512,256]{1,0:T(8,128)(2,1)S(1)}, bf16[512,256]{1,0:T(8,128)(2,1)}, u32[]{:S(2)}) copy-start(bf16[512,256]{1,0:T(8,128)(2,1)} %param.10) | copy-start | bytes 786436
  6.5 256.3 %all-gather.2.cloned.1.call-start = ((), (), s32[]{:S(2)}) async-start(), calls=%async_computation.7 | async-start | bytes 4456448 | tf_op jit(solution)/shard_map/all_gather | solution.py:92
  32.8 64.3 %all-to-all-start = ((bf16[8,1,128]{2,1,0:T(2,128)(2,1)}), bf16[8,1,128]{2,1,0:T(2,128)(2,1)S(1)}, u32[]{:S(2)}, u32[]{:S(2)}) async-start(bf16[8,1,128]{2,1,0:T(2,128)(2,1)} %copy.16), calls=%async_computation | async-start | bytes 8192 | tf_op jit(solution)/shard_map/all_to_all | solution.py:47
  39.1 73.3 %copy-start.5 = (bf16[8,256,128]{2,1,0:T(8,128)(2,1)S(1)}, bf16[8,256,128]{2,1,0:T(8,128)(2,1)}, u32[]{:S(2)}) copy-start(bf16[8,256,128]{2,1,0:T(8,128)(2,1)} %param.16) | copy-start | bytes 1572868
  97.1 15.3 %all-to-all-start.1 = ((bf16[8,128,256]{2,1,0:T(8,128)(2,1)}), bf16[8,128,256]{2,1,0:T(8,128)(2,1)S(1)}, u32[]{:S(2)}, u32[]{:S(2)}) async-start(bf16[8,128,256]{2,1,0:T(8,128)(2,1)} %scatter_fusion.1), calls=%async_computation.1 | async-start | bytes 1048576 | tf_op jit(solution)/shard_map/all_to_all | solution.py:46
  198.4 27.9 %all-to-all-start.2 = ((bf16[8,128,896]{2,1,0:T(8,128)(2,1)}), bf16[8,128,896]{2,1,0:T(8,128)(2,1)S(1)}, u32[]{:S(2)}, u32[]{:S(2)}) async-start(bf16[8,128,896]{2,1,0:T(8,128)(2,1)} %bitcast.68), calls=%async_computation.2 | async-start | bytes 3670016 | tf_op jit(solution)/shard_map/all_to_all | solution.py:77
  226.3 28.7 %all-to-all-start.3 = ((bf16[8,128,896]{2,1,0:T(8,128)(2,1)}), bf16[8,128,896]{2,1,0:T(8,128)(2,1)}, u32[]{:S(2)}, u32[]{:S(2)}) async-start(bf16[8,128,896]{2,1,0:T(8,128)(2,1)} %bitcast.67), calls=%async_computation.3 | async-start | bytes 3670016 | tf_op jit(solution)/shard_map/all_to_all | solution.py:84
  230.6 207.4 %all-reduce.3.cloned.1.call-start = ((), (), s32[]{:S(2)}) async-start(), calls=%async_computation.9 | async-start | bytes 262144 | tf_op jit(solution)/shard_map/psum | solution.py:105
  262.8 10.0 %copy-start.2 = (bf16[512,896]{1,0:T(8,128)(2,1)S(1)}, bf16[512,896]{1,0:T(8,128)(2,1)}, u32[]{:S(2)}) copy-start(bf16[512,896]{1,0:T(8,128)(2,1)} %gather_fusion) | copy-start | bytes 2752516
  262.9 10.0 %copy-start.4 = (bf16[512,4096]{1,0:T(8,128)(2,1)S(1)}, bf16[512,4096]{1,0:T(8,128)(2,1)}, u32[]{:S(2)}) copy-start(bf16[512,4096]{1,0:T(8,128)(2,1)} %all-gather.2.cloned.1.call-done) | copy-start | bytes 12582916
  358.8 1.2 copy-start.3
  359.7 159.4 %reduce-scatter.2.cloned.1.call-start = ((), (), s32[]{:S(2)}) async-start(), calls=%async_computation.8 | async-start | bytes 4456448 | tf_op jit(solution)/shard_map/reduce_scatter | solution.py:120
  369.3 68.7 %copy-start.6 = (bf16[8,64,256]{2,1,0:T(8,128)(2,1)S(1)}, bf16[8,64,256]{2,1,0:T(8,128)(2,1)}, u32[]{:S(2)}) copy-start(bf16[8,64,256]{2,1,0:T(8,128)(2,1)} %param.19) | copy-start | bytes 786436
Sparse Core Ops, SparseCore 0:
  9.4 59.1 all-gather.1
  359.8 78.1 all-reduce.2
  441.3 77.7 reduce-scatter.1
where the time goes:
time: 532 us; the launch traced here: 527 us
  waiting for transfers between devices  179 us (34%)
  local copies, waits for them, and re-layouts  150 us (28%)
  blocking collectives  122 us (23%)
  matrix products  39.9 us (8%)
  starting transfers between devices  18.8 us (4%)
  between operations  13.3 us (2%)
    scatter x3, local copies, waits for them, and re-layouts, pack(): return buffer.at[server, place].set(values)  129 us
    psum x1, blocking collectives, body(): ranks = lax.psum(part, 'tp').astype(jnp.bfloat16)  80.2 us
    psum x1, waiting for transfers between devices, body(): down_ranks = lax.psum(down_part.astype(jnp.bfloat16), 'tp')  68.7 us
    reduce_scatter x1, waiting for transfers between devices, body(): lax.psum_scatter(partial_value.astype(jnp.bfloat16), 'tp', scatter_dimens...  62 us
    all_to_all x1, blocking collectives, body(): lax.all_to_all(sent_hidden, 'grp', split_axis=0, concat_axis=0, tiled=True)  26.8 us
    all_to_all x1, waiting for transfers between devices, body(): lax.all_to_all(delta_gate.reshape(groups, capacity, hidden_share), 'grp',...  20.4 us
    all_to_all x1, waiting for transfers between devices, body(): lax.all_to_all(delta_up.reshape(groups, capacity, hidden_share), 'grp', s...  16.5 us
    all_to_all x1, blocking collectives, body(): lax.all_to_all(delta_down.reshape(groups, capacity, width_share), 'grp',...  14.6 us
  transfers between devices with their start and end apart: 7, of which 5 were waited for; matrix products, arithmetic and copies ran while one was open for 23% of the time, Pallas kernels for 0%

commit v1 on v0

v1 whole, which is shorter than its diff:
```python
import jax
import jax.numpy as jnp
from jax import lax
from jax.sharding import Mesh, PartitionSpec as P

GRP = ("z", "c")
TP = ("x", "y")
BF = jnp.bfloat16
F32 = jnp.float32


def dot(a, b):
    return jnp.dot(a, b, preferred_element_type=F32)


def sum_over(values, axis):
    n = lax.axis_size(axis)
    many = jnp.broadcast_to(values[None], (n,) + values.shape)
    got = lax.all_to_all(many, axis, split_axis=0, concat_axis=0, tiled=True)
    return jnp.sum(got.astype(F32), 0)


def sum_tp(values):
    first = sum_over(values.astype(BF), "x").astype(BF)
    return sum_over(first, "y").astype(BF)


def spread_onehot(onehot, vec):
    wide = onehot[:, :, None] * vec[:, None, :]
    return wide.reshape(vec.shape[0], -1)


def body(
    tokens,
    token_tenant,
    tenant_storage_slot,
    gate_matrix,
    up_matrix,
    down_matrix,
    adapter_gate_up_inputs,
    adapter_gate_up_outputs,
    adapter_down_inputs,
    adapter_down_outputs,
):
    groups = lax.axis_size(GRP)
    shares = lax.axis_size(TP)
    rows = tokens.shape[0]
    block_slots = adapter_gate_up_inputs.shape[0]
    rank = adapter_gate_up_inputs.shape[2] // 2
    hidden_share = gate_matrix.shape[1]
    width_share = tokens.shape[1]
    capacity = 2 * rows // groups
    table = jnp.arange(tenant_storage_slot.shape[0], dtype=jnp.int32)
    match = token_tenant[:, None] == table[None, :]
    slot = jnp.sum(jnp.where(match, tenant_storage_slot[None, :], 0), 1)
    server = slot // block_slots
    local = slot - server * block_slots
    picks = (server[:, None] == jnp.arange(groups, dtype=jnp.int32)[None, :]).astype(jnp.int32)
    place = jnp.sum(picks * (jnp.cumsum(picks, 0) - 1), 1)
    position = server * capacity + place
    seats = jnp.arange(groups * capacity, dtype=jnp.int32)
    seat_of = (seats[:, None] == position[None, :]).astype(BF)
    row_of = (position[:, None] == seats[None, :]).astype(BF)

    def exchange(values):
        got = lax.all_to_all(
            values.reshape((groups, -1) + values.shape[1:]),
            GRP,
            split_axis=0,
            concat_axis=0,
            tiled=True,
        )
        return got

    def pack(values):
        return dot(seat_of, values).astype(BF)

    extra = 16
    taken = jnp.sum(
        jnp.where(seats[:, None] == position[None, :], local[None, :] + 1, 0), 1
    ).astype(BF)
    notes = jnp.pad(
        taken.reshape(groups, 1, capacity),
        ((0, 0), (0, extra - 1), (0, width_share - capacity)),
    )
    sent = jnp.concatenate([pack(tokens).reshape(groups, capacity, width_share), notes], 1)
    got = exchange(sent.reshape(groups * (capacity + extra), width_share))
    rows_flattened = got[:, :capacity].reshape(groups * capacity, width_share)
    owner = got[:, capacity, :capacity].reshape(-1).astype(F32)
    onehot = (owner[:, None] == jnp.arange(1, block_slots + 1, dtype=F32)[None, :]).astype(BF)
    onehot_wide = onehot.astype(F32)[:, :, None]
    part = jnp.einsum("ny,eyq->neq", rows_flattened, adapter_gate_up_inputs, preferred_element_type=F32)
    part = jnp.sum(part * onehot_wide, 1)
    ranks = sum_tp(part)
    gate_factor = adapter_gate_up_outputs[:, :rank, :].reshape(block_slots * rank, hidden_share)
    up_factor = adapter_gate_up_outputs[:, rank:, :].reshape(block_slots * rank, hidden_share)
    delta_gate = dot(spread_onehot(onehot, ranks[:, :rank]), gate_factor).astype(BF)
    delta_up = dot(spread_onehot(onehot, ranks[:, rank:]), up_factor).astype(BF)
    back_gate = exchange(delta_gate).reshape(groups * capacity, hidden_share)
    back_up = exchange(delta_up).reshape(groups * capacity, hidden_share)
    piece = lax.all_gather(tokens, TP, axis=1, tiled=True)
    gate = dot(piece, gate_matrix) + dot(row_of, back_gate)
    up = dot(piece, up_matrix) + dot(row_of, back_up)
    hidden = (jax.nn.silu(gate) * up).astype(BF)
    got_hidden = exchange(pack(hidden)).reshape(groups * capacity, hidden_share)
    down_part = jnp.einsum("us,ysc->uyc", got_hidden, adapter_down_inputs, preferred_element_type=F32)
    down_part = jnp.sum(down_part * onehot_wide, 1)
    down_ranks = sum_tp(down_part)
    down_factor = adapter_down_outputs.reshape(block_slots * rank, width_share)
    delta_down = dot(spread_onehot(onehot, down_ranks), down_factor).astype(BF)
    back_down = exchange(delta_down).reshape(groups * capacity, width_share)
    partial = dot(hidden, down_matrix).astype(BF)
    split = partial.reshape(rows, shares, width_share).transpose(1, 0, 2)
    parts = lax.all_to_all(split, TP, split_axis=0, concat_axis=0, tiled=True)
    result = jnp.sum(parts.astype(F32), 0) + dot(row_of, back_down)
    return result.astype(BF)


def solution(mesh):
    sizes = mesh.devices.shape
    cores = 2
    side = 4
    fine = Mesh(
        mesh.devices.reshape(sizes[0] // cores, cores, sizes[1] // side, side),
        ("z", "c", "x", "y"),
    )
    return jax.shard_map(
        body,
        mesh=fine,
        in_specs=(
            P(GRP, TP),
            P(GRP),
            P(),
            P(None, TP),
            P(None, TP),
            P(TP, None),
            P(GRP, TP, None),
            P(GRP, None, TP),
            P(GRP, TP, None),
            P(GRP, None, TP),
        ),
        out_specs=P(GRP, TP),
        check_vma=False,
    )
```

time: 532 us -> 281 us (0.53)
  local copies, waits for them, and re-layouts: 150 us -> 4.21 us
  waiting for transfers between devices: 179 us -> 94 us
  blocking collectives: 122 us -> 85.4 us
  matrix products: 39.9 us -> 48.9 us
  starting transfers between devices: 18.8 us -> 26.5 us
    scatter x3 -> x0, local copies, waits for them, and re-layouts: 129 us -> none  [pack(): return buffer.at[server, place].set(values)]
    psum x1 -> x0, blocking collectives: 80.2 us -> none  [body(): ranks = lax.psum(part, 'tp').astype(jnp.bfloat16)]
    psum x1 -> x0, waiting for transfers between devices: 68.7 us -> none  [body(): down_ranks = lax.psum(down_part.astype(jnp.bfloat16), 'tp')]
    reduce_scatter x1 -> x0, waiting for transfers between devices: 62 us -> none  [body(): lax.psum_scatter(partial_value.astype(jnp.bfloat16), 'tp', scatter_dimens...]
    all_to_all x4 -> x6, waiting for transfers between devices: 47.1 us -> 93.3 us  [the longest x1 51.1 us: body(): parts = lax.all_to_all(split, TP, split_axis=0, concat_axis=0, tiled=True)]
    all_to_all x2 -> x4, blocking collectives: 41.4 us -> 85.4 us  [the longest x3 58.6 us: sum_over(): got = lax.all_to_all(many, axis, split_axis=0, concat_axis=0, tiled=True)]
    gather x3 -> x0, local copies, waits for them, and re-layouts: 18.7 us -> none  [the longest x1 7.85 us: body(): up = base_up + back_up[server, place].astype(jnp.float32)]
    dot_general x6 -> x11, matrix products: 36.9 us -> 45.9 us  [dot(): return jnp.dot(a, b, preferred_element_type=F32)]
  transfers between devices with their start and end apart: 7 -> 7, of which waited for: 5 -> 5; matrix products, arithmetic and copies ran while one was open for 23% -> 18% of each run, Pallas kernels for 0% -> 0%
where the time goes in v1:
time: 281 us; the launch traced here: 280 us
  waiting for transfers between devices  94 us (33%)
  blocking collectives  85.4 us (30%)
  matrix products  48.9 us (17%)
  starting transfers between devices  26.5 us (9%)
  between operations  13.6 us (5%)
  other arithmetic  7.11 us (3%)
  local copies, waits for them, and re-layouts  4.21 us (1%)
    all_to_all x3, blocking collectives, sum_over(): got = lax.all_to_all(many, axis, split_axis=0, concat_axis=0, tiled=True)  58.6 us
    all_to_all x1, waiting for transfers between devices, body(): parts = lax.all_to_all(split, TP, split_axis=0, concat_axis=0, tiled=True)  51.1 us
    dot_general x11, matrix products, dot(): return jnp.dot(a, b, preferred_element_type=F32)  45.9 us
    all_to_all x4, waiting for transfers between devices, exchange(): lax.all_to_all(values.reshape((groups, -1) + values.shape[1:]), GRP, spli...  42.2 us
    all_to_all x1, blocking collectives, exchange(): lax.all_to_all(values.reshape((groups, -1) + values.shape[1:]), GRP, spli...  26.8 us
    all_to_all x4, starting transfers between devices, exchange(): lax.all_to_all(values.reshape((groups, -1) + values.shape[1:]), GRP, spli...  17.1 us
    all_to_all x1, starting transfers between devices, body(): parts = lax.all_to_all(split, TP, split_axis=0, concat_axis=0, tiled=True)  5.7 us
  transfers between devices with their start and end apart: 7, of which 5 were waited for; matrix products, arithmetic and copies ran while one was open for 18% of the time, Pallas kernels for 0%

profile of v1, /device:TPU:0, one launch (start us, length us, event | category | flops | bytes accessed | tf_op | source)
XLA Modules:
  0.0 279.8 jit_solution(4216070812206038658)
XLA Ops:
  8.1 1.1 reduce-window.6
  9.9 1.5 fusion.6
  11.4 0.9 fusion.21
  12.3 5.4 %all-to-all-start = ((bf16[8,144,256]{2,1,0:T(8,128)(2,1)}), bf16[8,144,256]{2,1,0:T(8,128)(2,1)S(1)}, u32[]{:S(2)}, u32[]{:S(2)}) async-start(bf16[8,144,256]{2,1,0:T(8,128)(2,1)} %fusion.21), calls=%async_computation | async-start | bytes 1179648 | tf_op jit(solution)/shard_map/all_to_all | solution.py:66
  17.7 11.0 %all-to-all-done = bf16[8,144,256]{2,1,0:T(8,128)(2,1)S(1)} async-done(((bf16[8,144,256]{2,1,0:T(8,128)(2,1)}), bf16[8,144,256]{2,1,0:T(8,128)(2,1)S(1)}, u32[]{:S(2)}, u32[]{:S(2)}) %all-to-all-start) | async-done | bytes 589856 | tf_op jit(solution)/shard_map/all_to_all | solution.py:66
  28.9 1.8 multiply_reduce_fusion
  30.8 23.3 %all_to_all.50 = bf16[4,1024,128]{2,1,0:T(8,128)(2,1)S(1)} all-to-all(bf16[4,1024,128]{2,1,0:T(8,128)(2,1)S(1)} %broadcast_in_dim.36), channel_id=1, replica_groups=mesh['z'=4,'c'=2,'x'=4,'y'=4] {'x'}, dimensions={0} | all-to-all | bytes 2097152 | tf_op jit(solution)/shard_map/all_to_all | solution.py:19
  54.5 22.0 %all_to_all.51 = bf16[4,1024,128]{2,1,0:T(8,128)(2,1)S(1)} all-to-all(bf16[4,1024,128]{2,1,0:T(8,128)(2,1)S(1)} %broadcast_in_dim.37), channel_id=1, replica_groups=mesh['z'=4,'c'=2,'x'=4,'y'=4] {'y'}, dimensions={0} | all-to-all | bytes 2097152 | tf_op jit(solution)/shard_map/all_to_all | solution.py:19
  77.1 3.7 %bitcast_convert_fusion = bf16[1024,896]{1,0:T(8,128)(2,1)} fusion(bf16[8,128,896]{2,1,0:T(8,128)(2,1)} %param.17, bf16[1024,64]{0,1:T(8,128)(2,1)S(1)} %copy.18, bf16[1024,8]{0,1:T(8,128)(2,1)S(1)} %get-tuple-element.9), kind=kOutput, calls=%fused_computation.4 | convolution fusion | flops 940965888 | bytes 2899968 | tf_op jit(solution)/shard_map/dot_general | solution.py:13
  80.8 3.6 %all-to-all-start.4 = ((bf16[8,128,896]{2,1,0:T(8,128)(2,1)}), bf16[8,128,896]{2,1,0:T(8,128)(2,1)S(1)}, u32[]{:S(2)}, u32[]{:S(2)}) async-start(bf16[8,128,896]{2,1,0:T(8,128)(2,1)} %bitcast.78), calls=%async_computation.4 | async-start | bytes 3670016 | tf_op jit(solution)/shard_map/all_to_all | solution.py:66
  84.5 3.7 %bitcast_convert_fusion.1 = bf16[1024,896]{1,0:T(8,128)(2,1)} fusion(bf16[8,128,896]{2,1,0:T(8,128)(2,1)} %param.17, bf16[1024,64]{0,1:T(8,128)(2,1)S(1)} %copy.17, bf16[1024,8]{0,1:T(8,128)(2,1)S(1)} %get-tuple-element.9), kind=kOutput, calls=%fused_computation.5 | convolution fusion | flops 940965888 | bytes 2899968 | tf_op jit(solution)/shard_map/dot_general | solution.py:13
  88.3 20.4 %all-to-all-done.4 = bf16[8,128,896]{2,1,0:T(8,128)(2,1)S(1)} async-done(((bf16[8,128,896]{2,1,0:T(8,128)(2,1)}), bf16[8,128,896]{2,1,0:T(8,128)(2,1)S(1)}, u32[]{:S(2)}, u32[]{:S(2)}) %all-to-all-start.4) | async-done | bytes 1835040 | tf_op jit(solution)/shard_map/all_to_all | solution.py:66
  108.7 4.5 %all-to-all-start.3 = ((bf16[8,128,896]{2,1,0:T(8,128)(2,1)}), bf16[8,128,896]{2,1,0:T(8,128)(2,1)}, u32[]{:S(2)}, u32[]{:S(2)}) async-start(bf16[8,128,896]{2,1,0:T(8,128)(2,1)} %bitcast.77), calls=%async_computation.3 | async-start | bytes 3670016 | tf_op jit(solution)/shard_map/all_to_all | solution.py:66
  113.2 2.5 fusion.3
  115.7 10.3 %fusion.38 = f32[512,896]{1,0:T(8,128)} fusion(bf16[512,4096]{1,0:T(8,128)(2,1)} %all-gather.2.cloned.1.call-done, bf16[4096,896]{1,0:T(8,128)(2,1)} %param.14), kind=kOutput, calls=%fused_computation.74 | convolution fusion | flops 3758096384 | bytes 13369344 | tf_op jit(solution)/shard_map/dot_general | solution.py:13
  126.0 8.1 %fusion.37 = f32[512,896]{1,0:T(8,128)} fusion(bf16[512,4096]{1,0:T(8,128)(2,1)S(1)} %copy-done.1, bf16[4096,896]{1,0:T(8,128)(2,1)} %param.13), kind=kOutput, calls=%fused_computation.73 | convolution fusion | flops 3758096384 | bytes 13369344 | tf_op jit(solution)/shard_map/dot_general | solution.py:13
  134.1 3.3 %all-to-all-done.3 = bf16[8,128,896]{2,1,0:T(8,128)(2,1)} async-done(((bf16[8,128,896]{2,1,0:T(8,128)(2,1)}), bf16[8,128,896]{2,1,0:T(8,128)(2,1)}, u32[]{:S(2)}, u32[]{:S(2)}) %all-to-all-start.3) | async-done | bytes 1835040 | tf_op jit(solution)/shard_map/all_to_all | solution.py:66
  137.4 4.2 %multiply_convert_fusion = bf16[512,896]{1,0:T(8,128)(2,1)S(1)} fusion(f32[512,896]{1,0:T(8,128)} %fusion.38, f32[512,896]{1,0:T(8,128)S(1)} %copy-done.4, f32[512,896]{1,0:T(8,128)} %fusion.37, bf16[1024,896]{1,0:T(8,128)(2,1)} %bitcast.10, s32[512]{0:T(512)S(1)} %multiply_add_fusion), kind=kOutput, calls=%fused_computation.15 | convolution fusion | flops 943718400 | bytes 8259584 | tf_op jit(solution)/shard_map/dot_general | solution.py:13
  141.6 1.3 fusion.5
  142.9 26.8 %all_to_all.52 = bf16[8,128,896]{2,1,0:T(8,128)(2,1)S(1)} all-to-all(bf16[8,128,896]{2,1,0:T(8,128)(2,1)S(1)} %bitcast.80), channel_id=1, replica_groups=mesh['z'=4,'c'=2,'x'=4,'y'=4] {'z','c'}, dimensions={0} | all-to-all | bytes 3670016 | tf_op jit(solution)/shard_map/all_to_all | solution.py:66
  169.7 1.3 fusion.39
  171.3 13.3 %all_to_all.53 = bf16[4,1024,64]{1,2,0:T(8,128)(2,1)S(1)} all-to-all(bf16[4,1024,64]{1,2,0:T(8,128)(2,1)S(1)} %broadcast_in_dim.38), channel_id=1, replica_groups=mesh['z'=4,'c'=2,'x'=4,'y'=4] {'x'}, dimensions={0} | all-to-all | bytes 1048576 | tf_op jit(solution)/shard_map/all_to_all | solution.py:19
  185.5 3.7 %all-to-all-start.8 = ((bf16[4,1024,64]{1,2,0:T(8,128)(2,1)}), bf16[4,1024,64]{1,2,0:T(8,128)(2,1)S(1)}, u32[]{:S(2)}, u32[]{:S(2)}) async-start(bf16[4,1024,64]{1,2,0:T(8,128)(2,1)} %broadcast_in_dim.39), calls=%async_computation.8 | async-start | bytes 1048576 | tf_op jit(solution)/shard_map/all_to_all | solution.py:19
  189.2 8.0 %convolution_convert_fusion = bf16[512,4096]{1,0:T(8,128)(2,1)S(1)} fusion(bf16[512,896]{1,0:T(8,128)(2,1)S(1)} %copy-done.6, bf16[896,4096]{1,0:T(8,128)(2,1)} %param.15), kind=kOutput, calls=%fused_computation.1 | convolution fusion | flops 3760193536 | bytes 12451840 | tf_op jit(solution)/shard_map/dot_general | solution.py:13
  197.2 2.3 copy.23
  199.5 5.7 %all-to-all-start.5 = ((bf16[16,512,256]{2,1,0:T(8,128)(2,1)}), bf16[16,512,256]{2,1,0:T(8,128)(2,1)}, u32[]{:S(2)}, u32[]{:S(2)}) async-start(bf16[16,512,256]{2,1,0:T(8,128)(2,1)} %bitcast.73), calls=%async_computation.5 | async-start | bytes 8388608 | tf_op jit(solution)/shard_map/all_to_all | solution.py:114
  205.4 1.3 fusion.7
  206.7 51.1 %all-to-all-done.5 = bf16[16,512,256]{2,1,0:T(8,128)(2,1)} async-done(((bf16[16,512,256]{2,1,0:T(8,128)(2,1)}), bf16[16,512,256]{2,1,0:T(8,128)(2,1)}, u32[]{:S(2)}, u32[]{:S(2)}) %all-to-all-start.5) | async-done | bytes 4194336 | tf_op jit(solution)/shard_map/all_to_all | solution.py:114
  257.8 3.6 %all-to-all-start.9 = ((bf16[8,128,256]{2,1,0:T(8,128)(2,1)}), bf16[8,128,256]{2,1,0:T(8,128)(2,1)S(1)}, u32[]{:S(2)}, u32[]{:S(2)}) async-start(bf16[8,128,256]{2,1,0:T(8,128)(2,1)} %bitcast.21), calls=%async_computation.9 | async-start | bytes 1048576 | tf_op jit(solution)/shard_map/all_to_all | solution.py:66
  261.4 2.8 %convert_reduce_fusion = f32[512,256]{1,0:T(8,128)S(1)} fusion(bf16[16,512,256]{2,1,0:T(8,128)(2,1)} %all-to-all-done.5), kind=kLoop, calls=%fused_computation | loop fusion | flops 4063232 | bytes 4718592 | tf_op jit(solution)/shard_map/reduce_sum | solution.py:115
  264.2 7.5 %all-to-all-done.9 = bf16[8,128,256]{2,1,0:T(8,128)(2,1)S(1)} async-done(((bf16[8,128,256]{2,1,0:T(8,128)(2,1)}), bf16[8,128,256]{2,1,0:T(8,128)(2,1)S(1)}, u32[]{:S(2)}, u32[]{:S(2)}) %all-to-all-start.9) | async-done | bytes 524320 | tf_op jit(solution)/shard_map/all_to_all | solution.py:66
  271.7 1.2 fusion.9
  (46 shorter events, 4.9 us)
Async XLA Ops:
  6.5 163.2 %copy-start = (bf16[8,896,64]{1,2,0:T(8,128)(2,1)S(1)}, bf16[8,896,64]{1,2,0:T(8,128)(2,1)}, u32[]{:S(2)}) copy-start(bf16[8,896,64]{1,2,0:T(8,128)(2,1)} %param.18) | copy-start | bytes 2752516
  6.5 109.2 %all-gather.2.cloned.1.call-start = ((), (), s32[]{:S(2)}) async-start(), calls=%async_computation.10 | async-start | bytes 4456448 | tf_op jit(solution)/shard_map/all_gather | solution.py:101
  9.9 18.9 %copy-start.2 = (bf16[8,256,128]{2,1,0:T(8,128)(2,1)S(1)}, bf16[8,256,128]{2,1,0:T(8,128)(2,1)}, u32[]{:S(2)}) copy-start(bf16[8,256,128]{2,1,0:T(8,128)(2,1)} %param.16) | copy-start | bytes 1572868
  12.3 16.5 %all-to-all-start = ((bf16[8,144,256]{2,1,0:T(8,128)(2,1)}), bf16[8,144,256]{2,1,0:T(8,128)(2,1)S(1)}, u32[]{:S(2)}, u32[]{:S(2)}) async-start(bf16[8,144,256]{2,1,0:T(8,128)(2,1)} %fusion.21), calls=%async_computation | async-start | bytes 1179648 | tf_op jit(solution)/shard_map/all_to_all | solution.py:66
  80.8 27.9 %all-to-all-start.4 = ((bf16[8,128,896]{2,1,0:T(8,128)(2,1)}), bf16[8,128,896]{2,1,0:T(8,128)(2,1)S(1)}, u32[]{:S(2)}, u32[]{:S(2)}) async-start(bf16[8,128,896]{2,1,0:T(8,128)(2,1)} %bitcast.78), calls=%async_computation.4 | async-start | bytes 3670016 | tf_op jit(solution)/shard_map/all_to_all | solution.py:66
  108.7 28.7 %all-to-all-start.3 = ((bf16[8,128,896]{2,1,0:T(8,128)(2,1)}), bf16[8,128,896]{2,1,0:T(8,128)(2,1)}, u32[]{:S(2)}, u32[]{:S(2)}) async-start(bf16[8,128,896]{2,1,0:T(8,128)(2,1)} %bitcast.77), calls=%async_computation.3 | async-start | bytes 3670016 | tf_op jit(solution)/shard_map/all_to_all | solution.py:66
  115.7 10.3 %copy-start.1 = (bf16[512,4096]{1,0:T(8,128)(2,1)S(1)}, bf16[512,4096]{1,0:T(8,128)(2,1)}, u32[]{:S(2)}) copy-start(bf16[512,4096]{1,0:T(8,128)(2,1)} %all-gather.2.cloned.1.call-done) | copy-start | bytes 12582916
  126.0 11.4 %copy-start.4 = (f32[512,896]{1,0:T(8,128)S(1)}, f32[512,896]{1,0:T(8,128)}, u32[]{:S(2)}) copy-start(f32[512,896]{1,0:T(8,128)} %fusion.3) | copy-start | bytes 5505028
  141.6 1.3 copy-start.5
  171.2 18.0 %copy-start.6 = (bf16[512,896]{1,0:T(8,128)(2,1)S(1)}, bf16[512,896]{1,0:T(8,128)(2,1)}, u32[]{:S(2)}) copy-start(bf16[512,896]{1,0:T(8,128)(2,1)} %copy-done.5) | copy-start | bytes 2752516
  185.5 14.0 %all-to-all-start.8 = ((bf16[4,1024,64]{1,2,0:T(8,128)(2,1)}), bf16[4,1024,64]{1,2,0:T(8,128)(2,1)S(1)}, u32[]{:S(2)}, u32[]{:S(2)}) async-start(bf16[4,1024,64]{1,2,0:T(8,128)(2,1)} %broadcast_in_dim.39), calls=%async_computation.8 | async-start | bytes 1048576 | tf_op jit(solution)/shard_map/all_to_all | solution.py:19
  199.5 5.8 %copy-start.3 = (bf16[8,64,256]{2,1,0:T(8,128)(2,1)S(1)}, bf16[8,64,256]{2,1,0:T(8,128)(2,1)}, u32[]{:S(2)}) copy-start(bf16[8,64,256]{2,1,0:T(8,128)(2,1)} %param.19) | copy-start | bytes 786436
  199.5 58.3 %all-to-all-start.5 = ((bf16[16,512,256]{2,1,0:T(8,128)(2,1)}), bf16[16,512,256]{2,1,0:T(8,128)(2,1)}, u32[]{:S(2)}, u32[]{:S(2)}) async-start(bf16[16,512,256]{2,1,0:T(8,128)(2,1)} %bitcast.73), calls=%async_computation.5 | async-start | bytes 8388608 | tf_op jit(solution)/shard_map/all_to_all | solution.py:114
  257.8 13.9 %all-to-all-start.9 = ((bf16[8,128,256]{2,1,0:T(8,128)(2,1)}), bf16[8,128,256]{2,1,0:T(8,128)(2,1)S(1)}, u32[]{:S(2)}, u32[]{:S(2)}) async-start(bf16[8,128,256]{2,1,0:T(8,128)(2,1)} %bitcast.21), calls=%async_computation.9 | async-start | bytes 1048576 | tf_op jit(solution)/shard_map/all_to_all | solution.py:66
Sparse Core Ops, SparseCore 0:
  9.4 66.9 all-gather.1

commit v2 on v1

v2 whole, which is shorter than its diff:
```python
import functools

import jax
import jax.numpy as jnp
from jax import lax
from jax.experimental import pallas as pl
from jax.experimental.pallas import tpu as pltpu
from jax.sharding import Mesh, PartitionSpec as P

GRP = ("z", "c")
TP = ("x", "y")
BF = jnp.bfloat16
F32 = jnp.float32
FAN = 4


def dot(a, b):
    return jnp.dot(a, b, preferred_element_type=F32)


def dot_bf(a, b):
    return dot(a, b).astype(BF)


def shift(values, axis, step):
    n = lax.axis_size(axis)
    return lax.ppermute(values, axis, [(i, (i + step) % n) for i in range(n)])


def swap(values):
    return shift(values, "c", 1)


def over_tp(values):
    return lax.all_to_all(values, TP, split_axis=0, concat_axis=0, tiled=True)


def sum_over(values, axis):
    got = [shift(values, axis, step).astype(F32) for step in (1, -1, 2)]
    return ((values.astype(F32) + got[0]) + (got[1] + got[2])).astype(BF)


def sum_tp_steps(values):
    first = sum_over(values, "x")
    return sum_over(first, "y")


def sum_tp_parts(values):
    shares = lax.axis_size(TP)
    rows, width = values.shape
    got = over_tp(values.reshape(shares, rows // shares, width))
    own = jnp.sum(got.astype(F32), 0).astype(BF)
    return over_tp(jnp.broadcast_to(own[None], (shares,) + own.shape)).reshape(rows, width)


def ring(first, second):
    below = (shift(first, "z", 1), shift(second, "z", 1))
    above = (shift(first, "z", -1), shift(second, "z", -1))
    far = (shift(below[0], "z", 1), shift(above[1], "z", -1))
    return [(first, second), below, above, far]


def base_kernel(tokens_ref, w_ref, out_ref):
    tokens = jnp.concatenate([tokens_ref[i] for i in range(tokens_ref.shape[0])], 1)
    product = dot(tokens, w_ref[...])
    first = pl.program_id(0) == 0

    @pl.when(first)
    def _():
        out_ref[...] = product

    @pl.when(jnp.logical_not(first))
    def _():
        out_ref[...] += product


def base_product(pieces, matrix):
    shares, rows, share = pieces.shape
    width = matrix.shape[1]
    return pl.pallas_call(
        base_kernel,
        grid=(shares // FAN,),
        in_specs=[
            pl.BlockSpec((FAN, rows, share), lambda k: (k, 0, 0)),
            pl.BlockSpec((FAN * share, width), lambda k: (k, 0)),
        ],
        out_specs=pl.BlockSpec((rows, width), lambda k: (0, 0)),
        out_shape=jax.ShapeDtypeStruct((rows, width), F32),
        name="base",
        cost_estimate=pl.CostEstimate(
            flops=2 * rows * share * shares * width,
            bytes_accessed=2 * share * shares * width + 6 * rows * width,
            transcendentals=0,
        ),
    )(pieces, matrix)


def down_kernel(hidden_ref, w_ref, out_ref):
    product = dot_bf(hidden_ref[...], w_ref[...])
    share = out_ref.shape[2]
    for i in range(out_ref.shape[0]):
        out_ref[i] = product[:, i * share : (i + 1) * share]


def down_product(hidden, matrix, shares):
    rows, depth = hidden.shape
    share = matrix.shape[1] // shares
    return pl.pallas_call(
        down_kernel,
        grid=(shares // FAN,),
        in_specs=[
            pl.BlockSpec((rows, depth), lambda k: (0, 0)),
            pl.BlockSpec((depth, FAN * share), lambda k: (0, k)),
        ],
        out_specs=pl.BlockSpec((FAN, rows, share), lambda k: (k, 0, 0)),
        out_shape=jax.ShapeDtypeStruct((shares, rows, share), BF),
        name="partial",
        cost_estimate=pl.CostEstimate(
            flops=2 * rows * depth * share * shares,
            bytes_accessed=2 * (depth + rows) * share * shares + 2 * rows * depth,
            transcendentals=0,
        ),
    )(hidden, matrix)


def fan_out(start, depth, rank, slots):
    lane = lax.broadcasted_iota(jnp.int32, (depth, slots * rank), 1)
    row = lax.broadcasted_iota(jnp.int32, (depth, slots * rank), 0)
    return (row == lax.rem(lane, rank) + start).astype(BF)


def slot_mask(local, rows, rank, first, slots):
    lane = lax.broadcasted_iota(jnp.int32, (rows, slots * rank), 1) // rank + first
    return local.astype(F32).astype(jnp.int32) == lane


def split_rows(values, own_ref, other_ref, i):
    half = values.shape[0] // 2
    rows = pl.ds(i * half, half)
    return (own_ref, rows, values[:half]), (other_ref, rows, values[half:])


def delta_kernel(count, rank, *refs):
    ranks_ref, local_ref = refs[:2]
    factors = refs[2 : 2 + 2 * count]
    own_ref, other_ref = refs[2 + 2 * count :]
    slots = factors[0].shape[0]
    width = factors[0].shape[2]
    rows = ranks_ref.shape[1]
    for which in range(2):
        fan = fan_out(which * rank, ranks_ref.shape[2], rank, slots)
        for i in range(count):
            wide = dot(ranks_ref[i], fan)
            wide = jnp.where(slot_mask(local_ref[i], rows, rank, 0, slots), wide, 0.0).astype(BF)
            delta = dot_bf(wide, factors[2 * i + which][...].reshape(slots * rank, width))
            for ref, at, part in split_rows(delta, own_ref, other_ref, i):
                ref[at, which * width : (which + 1) * width] = part


def down_rank_kernel(count, rank, *refs):
    hidden_ref, local_ref = refs[:2]
    factors = refs[2 : 2 + 2 * count]
    own_ref, other_ref = refs[2 + 2 * count :]
    slots = factors[0].shape[0]
    rows, depth = hidden_ref.shape[1:]
    fan = fan_out(0, rank, rank, slots)
    for i in range(count):
        total = jnp.zeros((rows, rank), F32)
        for which in range(2):
            factor = factors[2 * i + which][:, :, :depth].reshape(slots * rank, depth)
            part = lax.dot_general(
                hidden_ref[i], factor, (((1,), (1,)), ((), ())), preferred_element_type=F32
            )
            mask = slot_mask(local_ref[i], rows, rank, which * slots, slots)
            part = jnp.where(mask, part, 0.0).astype(BF)
            total += lax.dot_general(part, fan, (((1,), (1,)), ((), ())), preferred_element_type=F32)
        for ref, at, part in split_rows(total.astype(BF), own_ref, other_ref, i):
            ref[at, :] = part


def down_delta_kernel(count, rank, *refs):
    ranks_ref, local_ref = refs[:2]
    factors = refs[2 : 2 + 2 * count]
    own_ref, other_ref = refs[2 + 2 * count :]
    slots = factors[0].shape[0]
    rows = ranks_ref.shape[1]
    width = own_ref.shape[1]
    fan = fan_out(0, rank, rank, slots)
    for i in range(count):
        total = jnp.zeros((rows, width), F32)
        spread = dot(ranks_ref[i], fan)
        for which in range(2):
            mask = slot_mask(local_ref[i], rows, rank, which * slots, slots)
            wide = jnp.where(mask, spread, 0.0).astype(BF)
            factor = factors[2 * i + which]
            factor = factor[:, :, factor.shape[2] - width :].reshape(slots * rank, width)
            total += dot(wide, factor)
        for ref, at, part in split_rows(total.astype(BF), own_ref, other_ref, i):
            ref[at, :] = part


def seated_call(kernel, rank, seated, local, factors, width, flops):
    count, rows = seated.shape[:2]
    out = jax.ShapeDtypeStruct((count * rows // 2, width), BF)
    flat = [f for pair in factors for f in pair]
    moved = sum(2 * f.size for f in flat) + 4 * out.size + 2 * seated.size
    return pl.pallas_call(
        functools.partial(kernel, count, rank),
        in_specs=[pl.BlockSpec(memory_space=pltpu.VMEM)] * (2 + len(flat)),
        out_specs=[pl.BlockSpec(memory_space=pltpu.VMEM)] * 2,
        out_shape=[out, out],
        cost_estimate=pl.CostEstimate(flops=flops, bytes_accessed=moved, transcendentals=0),
    )(seated, local, *flat)


def layer(
    tokens,
    token_tenant,
    tenant_storage_slot,
    gate_matrix,
    up_matrix,
    down_matrix,
    adapter_gate_up_inputs,
    adapter_gate_up_outputs,
    adapter_down_inputs,
    adapter_down_outputs,
):
    groups = lax.axis_size(GRP)
    shares = lax.axis_size(TP)
    rows = tokens.shape[0]
    block_slots = adapter_gate_up_inputs.shape[0]
    rank = adapter_gate_up_inputs.shape[2] // 2
    hidden_share = gate_matrix.shape[1]
    width_share = tokens.shape[1]
    capacity = 2 * rows // groups
    chips = groups // 2
    side = chips * capacity
    near = (chips - 1) * capacity

    in_factors = [adapter_gate_up_inputs]
    in_factors += [shift(adapter_gate_up_inputs, "z", step) for step in (1, -1, 2)]
    pieces = over_tp(jnp.broadcast_to(tokens[None], (shares,) + tokens.shape))
    gate_part = adapter_gate_up_outputs[:, :rank, :]
    up_part = adapter_gate_up_outputs[:, rank:, :]
    out_factors = ring(gate_part, up_part)
    down_in = adapter_down_inputs.swapaxes(1, 2)
    half = block_slots // 2
    low = jnp.concatenate([down_in[:half], adapter_down_outputs[:half]], 2)
    high = jnp.concatenate([down_in[half:], adapter_down_outputs[half:]], 2)
    down_factors = ring(low, high)
    base_gate = base_product(pieces, gate_matrix)
    base_up = base_product(pieces, up_matrix)

    tokens_pair = (tokens, swap(tokens))
    tenants = jnp.stack([token_tenant, swap(token_tenant)])
    table = jnp.arange(tenant_storage_slot.shape[0], dtype=jnp.int32)
    match = tenants[:, :, None] == table[None, None, :]
    slot = jnp.sum(jnp.where(match, tenant_storage_slot[None, None, :], 0), 2)
    server = slot // block_slots
    local = slot - server * block_slots
    picks = (server[:, :, None] == jnp.arange(groups, dtype=jnp.int32)).astype(jnp.int32)
    place = jnp.sum(picks * (jnp.cumsum(picks, 1) - 1), 2)
    apart = lax.rem(server // 2 - lax.axis_index("z") + chips, chips)
    turn = jnp.where(apart == 0, 0, jnp.where(apart == chips - 1, 1, jnp.where(apart == 1, 2, 3)))
    seat = turn * capacity + place
    mine = lax.rem(server, 2) == lax.axis_index("c")
    here = jnp.where(mine, seat, -1)
    there = jnp.where(mine, -1, seat)[0]
    seats = jnp.arange(side, dtype=jnp.int32)
    take = (seats[None, :, None] == here[:, None, :]).astype(BF)
    give_here = (here[0][:, None] == seats[None, :]).astype(BF)
    give_there = (there[:, None] == seats[None, :]).astype(BF)

    def by_block(pair):
        packed = [dot_bf(take[g], v).reshape(chips, capacity, -1) for g, v in enumerate(pair)]
        return jnp.concatenate(packed, 1)

    def home(own, other, start):
        stop = start + own.shape[0]
        return dot(give_here[:, start:stop], own) + dot(give_there[:, start:stop], other)

    seat_local = by_block((local[0][:, None].astype(BF), local[1][:, None].astype(BF)))

    seated = by_block(tokens_pair)
    chosen = seat_local.astype(F32) == jnp.arange(block_slots, dtype=F32)[None, None, :]
    parts = []
    for i, f in enumerate(in_factors):
        part = jnp.einsum("ny,eyq->neq", seated[i], f, preferred_element_type=F32)
        parts.append(jnp.sum(part * chosen[i].astype(F32)[:, :, None], 1).astype(BF))
    own = jnp.concatenate([o[:capacity] for o in parts], 0)
    other = swap(jnp.concatenate([o[capacity:] for o in parts], 0))
    home_part = home(own, other, 0).astype(BF)
    ranks = sum_tp_parts(home_part)
    seated_ranks = by_block((ranks, swap(ranks)))

    def deltas(first, last):
        count = last - first
        flops = 4 * 2 * capacity * count * block_slots * rank * hidden_share
        return seated_call(
            delta_kernel,
            rank,
            seated_ranks[first:last],
            seat_local[first:last],
            out_factors[first:last],
            2 * hidden_share,
            flops,
        )

    own, other = deltas(0, chips - 1)
    other = swap(other)
    gate = base_gate + home(own[:, :hidden_share], other[:, :hidden_share], 0)
    up = base_up + home(own[:, hidden_share:], other[:, hidden_share:], 0)
    own, other = deltas(chips - 1, chips)
    other = swap(other)
    gate = gate + home(own[:, :hidden_share], other[:, :hidden_share], near)
    up = up + home(own[:, hidden_share:], other[:, hidden_share:], near)
    hidden = (jax.nn.silu(gate) * up).astype(BF)

    partial = down_product(hidden, down_matrix, shares)
    hidden_pair = (hidden, swap(hidden))
    summed = over_tp(partial)

    seated_hidden = by_block(hidden_pair)
    flops = 4 * side * block_slots * rank * hidden_share
    own, other = seated_call(
        down_rank_kernel, rank, seated_hidden, seat_local, down_factors, rank, flops
    )
    down_rows = home(own, swap(other), 0).astype(BF)
    down_ranks = sum_tp_steps(down_rows)
    seated_down = by_block((down_ranks, swap(down_ranks)))
    flops = 4 * side * block_slots * rank * width_share
    own, other = seated_call(
        down_delta_kernel, rank, seated_down, seat_local, down_factors, width_share, flops
    )
    returned = home(own, swap(other), 0)
    return (jnp.sum(summed.astype(F32), 0) + returned).astype(BF)


def solution(mesh):
    sizes = mesh.devices.shape
    cores = 2
    side = 4
    fine = Mesh(
        mesh.devices.reshape(sizes[0] // cores, cores, sizes[1] // side, side),
        ("z", "c", "x", "y"),
    )
    return jax.shard_map(
        layer,
        mesh=fine,
        in_specs=(
            P(GRP, TP),
            P(GRP),
            P(),
            P(None, TP),
            P(None, TP),
            P(TP, None),
            P(GRP, TP, None),
            P(GRP, None, TP),
            P(GRP, TP, None),
            P(GRP, None, TP),
        ),
        out_specs=P(GRP, TP),
        check_vma=False,
    )
```

time: 281 us -> 266 us (0.947); the launches traced: 280 us -> 261 us
  blocking collectives: 85.4 us -> 14.7 us
  Pallas kernels: 0 us -> 47 us
  starting transfers between devices: 26.5 us -> 53.7 us
  matrix products: 48.9 us -> 34.4 us
  between operations: 13.6 us -> 0.69 us
  local copies, waits for them, and re-layouts: 4.21 us -> 9.77 us
  waiting for transfers between devices: 94 us -> 89.6 us
  other arithmetic: 7.11 us -> 11.3 us
    all_to_all x6 -> x3, waiting for transfers between devices: 93.3 us -> 0.27 us  [over_tp(): return lax.all_to_all(values, TP, split_axis=0, concat_axis=0, tiled=True)]
    ppermute x0 -> x31, waiting for transfers between devices: none -> 89.3 us  [shift(): return lax.ppermute(values, axis, [(i, (i + step) % n) for i in range(n)])]
    all_to_all x4 -> x1, blocking collectives: 85.4 us -> 14.7 us  [over_tp(): return lax.all_to_all(values, TP, split_axis=0, concat_axis=0, tiled=True)]
    pallas_call x0 -> x7, Pallas kernels: none -> 47 us  [the longest x4 20 us: seated_call(): pl.pallas_call(functools.partial(kernel, count, rank), in_specs=[pl.Block...]
    ppermute x0 -> x31, starting transfers between devices: none -> 36.1 us  [shift(): return lax.ppermute(values, axis, [(i, (i + step) % n) for i in range(n)])]
    dot_general x11 -> x24, matrix products: 45.9 us -> 33 us  [dot(): return jnp.dot(a, b, preferred_element_type=F32)]
    all_to_all x6 -> x3, starting transfers between devices: 26.5 us -> 17.6 us  [over_tp(): return lax.all_to_all(values, TP, split_axis=0, concat_axis=0, tiled=True)]
    slice x5 -> x11, local copies, waits for them, and re-layouts: 0.64 us -> 5.27 us  [the longest x2 1.97 us: layer(): high = jnp.concatenate([down_in[half:], adapter_down_outputs[half:]], 2)]
  transfers between devices with their start and end apart: 7 -> 34, of which waited for: 5 -> 16; matrix products, arithmetic and copies ran while one was open for 18% -> 16% of each run, Pallas kernels for 0% -> 8%
where the time goes in v2:
time: 266 us; the launch traced here: 261 us
  waiting for transfers between devices  89.6 us (34%)
  starting transfers between devices  53.7 us (20%)
  Pallas kernels  47 us (18%)
  matrix products  34.4 us (13%)
  blocking collectives  14.7 us (6%)
  other arithmetic  11.3 us (4%)
  local copies, waits for them, and re-layouts  9.77 us (4%)
    ppermute x31, waiting for transfers between devices, shift(): return lax.ppermute(values, axis, [(i, (i + step) % n) for i in range(n)])  89.3 us
    ppermute x31, starting transfers between devices, shift(): return lax.ppermute(values, axis, [(i, (i + step) % n) for i in range(n)])  36.1 us
    dot_general x24, matrix products, dot(): return jnp.dot(a, b, preferred_element_type=F32)  33 us
    pallas_call x4, Pallas kernels, seated_call(): pl.pallas_call(functools.partial(kernel, count, rank), in_specs=[pl.Block...  20 us
    pallas_call x2, Pallas kernels, base_product(): pl.pallas_call(base_kernel, grid=(shares // FAN,), in_specs=[pl.BlockSpec...  18.4 us
    all_to_all x3, starting transfers between devices, over_tp(): return lax.all_to_all(values, TP, split_axis=0, concat_axis=0, tiled=True)  17.6 us
    all_to_all x1, blocking collectives, over_tp(): return lax.all_to_all(values, TP, split_axis=0, concat_axis=0, tiled=True)  14.7 us
    pallas_call x1, Pallas kernels, down_product(): pl.pallas_call(down_kernel, grid=(shares // FAN,), in_specs=[pl.BlockSpec...  8.59 us
  transfers between devices with their start and end apart: 34, of which 16 were waited for; matrix products, arithmetic and copies ran while one was open for 16% of the time, Pallas kernels for 8%

profile of v2, /device:TPU:0, one launch (start us, length us, event | category | flops | bytes accessed | tf_op | source)
XLA Modules:
  0.0 261.1 jit_solution(6706609579032232411)
XLA Ops:
  0.0 4.1 %collective-permute-start.4 = (bf16[8,256,128]{2,1,0:T(8,128)(2,1)}, bf16[8,256,128]{2,1,0:T(8,128)(2,1)S(1)}, u32[]{:S(2)}, u32[]{:S(2)}) collective-permute-start(bf16[8,256,128]{2,1,0:T(8,128)(2,1)} %param.16), channel_id=1, source_target_pairs={{0,64},{32,96},{64,0},{96,32},{1,65},{33,97},{65,1},{97,33},{2,66}... | collective-permute-start | bytes 1572872 | tf_op jit(solution)/shard_map/ppermute | solution.py:27
  12.4 16.4 %collective-permute-done.3 = bf16[8,256,128]{2,1,0:T(8,128)(2,1)S(1)} collective-permute-done((bf16[8,256,128]{2,1,0:T(8,128)(2,1)}, bf16[8,256,128]{2,1,0:T(8,128)(2,1)S(1)}, u32[]{:S(2)}, u32[]{:S(2)}) %collective-permute-start.3) | collective-permute-done | bytes 524320 | tf_op jit(solution)/shard_map/ppermute | solution.py:27
  31.8 14.7 %all_to_all.20 = bf16[16,32,128]{2,1,0:T(8,128)(2,1)S(1)} all-to-all(bf16[16,32,128]{2,1,0:T(8,128)(2,1)S(1)} %bitcast.103), channel_id=1, replica_groups=mesh['z'=4,'c'=2,'x'=4,'y'=4] {'x','y'}, dimensions={0} | all-to-all | bytes 262144 | tf_op jit(solution)/shard_map/all_to_all | solution.py:35
  47.2 3.6 %all-to-all-start.2 = ((bf16[16,32,128]{2,1,0:T(8,128)(2,1)}), bf16[16,32,128]{2,1,0:T(8,128)(2,1)S(1)}, u32[]{:S(2)}, u32[]{:S(2)}) async-start(bf16[16,32,128]{2,1,0:T(8,128)(2,1)} %broadcast_in_dim.30), calls=%async_computation.2 | async-start | bytes 262144 | tf_op jit(solution)/shard_map/all_to_all | solution.py:35
  52.4 2.7 %collective-permute-start.10 = (bf16[8,64,896]{2,1,0:T(8,128)(2,1)S(1)}, bf16[8,64,896]{2,1,0:T(8,128)(2,1)}, u32[]{:S(2)}, u32[]{:S(2)}) collective-permute-start(bf16[8,64,896]{2,1,0:T(8,128)(2,1)S(1)} %get-tuple-element.26.refs_3_), channel_id=1, source_target_pairs={{0,96},{32,0},{64,32},{96,64},{1,97},{33,1},{65,33},{97,65},{2,98}... | collective-permute-start | bytes 2752520 | tf_op jit(solution)/shard_map/ppermute | solution.py:27
  55.1 3.3 %collective-permute-start.9 = (bf16[8,64,896]{2,1,0:T(8,128)(2,1)S(1)}, bf16[8,64,896]{2,1,0:T(8,128)(2,1)}, u32[]{:S(2)}, u32[]{:S(2)}) collective-permute-start(bf16[8,64,896]{2,1,0:T(8,128)(2,1)S(1)} %get-tuple-element.27.refs_2_), channel_id=1, source_target_pairs={{0,96},{32,0},{64,32},{96,64},{1,97},{33,1},{65,33},{97,65},{2,98}... | collective-permute-start | bytes 2752520 | tf_op jit(solution)/shard_map/ppermute | solution.py:27
  61.1 7.1 %all-to-all-start = ((bf16[16,512,256]{2,1,0:T(8,128)(2,1)}), bf16[16,512,256]{2,1,0:T(8,128)(2,1)}, u32[]{:S(2)}, u32[]{:S(2)}) async-start(bf16[16,512,256]{2,1,0:T(8,128)(2,1)} %broadcast_in_dim.27), calls=%async_computation | async-start | bytes 8388608 | tf_op jit(solution)/shard_map/all_to_all | solution.py:35
  72.4 24.4 %collective-permute-done.7.refs_4_ = bf16[8,64,896]{2,1,0:T(8,128)(2,1)} collective-permute-done((bf16[8,64,896]{2,1,0:T(8,128)(2,1)S(1)}, bf16[8,64,896]{2,1,0:T(8,128)(2,1)}, u32[]{:S(2)}, u32[]{:S(2)}) %collective-permute-start.7) | collective-permute-done | bytes 917536 | tf_op jit(solution)/shard_map/ppermute | solution.py:27
  96.8 3.2 %collective-permute-start.13 = (bf16[8,64,896]{2,1,0:T(8,128)(2,1)}, bf16[8,64,896]{2,1,0:T(8,128)(2,1)}, u32[]{:S(2)}, u32[]{:S(2)}) collective-permute-start(bf16[8,64,896]{2,1,0:T(8,128)(2,1)} %collective-permute-done.10.refs_7_), channel_id=1, source_target_pairs={{0,96},{32,0},{64,32},{96,64},{1,97},{33,1},{65,33},{97,65},{2,98}... | collective-permute-start | bytes 2752520 | tf_op jit(solution)/shard_map/ppermute | solution.py:27
  103.5 7.0 %shard_map.100 = (bf16[384,1792]{1,0:T(8,128)(2,1)}, bf16[384,1792]{1,0:T(8,128)(2,1)}) custom-call(bf16[3,256,128]{2,1,0:T(8,128)(2,1)} %fusion.40.refs_0_, bf16[3,256,1]{2,1,0:T(8,128)(2,1)} %slice.228.refs_1_, bf16[8,64,896]{2,1,0:T(8,128)(2,1)} %copy-done.4, bf16[8,64,896]{2,1,0:T(8,128)(2,1)} %copy-done.3, ...), custom_call_target="tpu_custom_call" | custom-call | flops 1409286144 | bytes 8454144 | tf_op jit(solution)/shard_map/pallas_call | solution.py:207
  112.9 5.2 %collective-permute-done.12.refs_2_ = bf16[8,64,896]{2,1,0:T(8,128)(2,1)} collective-permute-done((bf16[8,64,896]{2,1,0:T(8,128)(2,1)}, bf16[8,64,896]{2,1,0:T(8,128)(2,1)}, u32[]{:S(2)}, u32[]{:S(2)}) %collective-permute-start.12) | collective-permute-done | bytes 917536 | tf_op jit(solution)/shard_map/ppermute | solution.py:27
  118.2 3.4 %shard_map.101 = (bf16[128,1792]{1,0:T(8,128)(2,1)}, bf16[128,1792]{1,0:T(8,128)(2,1)}) custom-call(bf16[1,256,128]{2,1,0:T(8,128)(2,1)} %pad_maximum_fusion.6.refs_0_, bf16[1,256,1]{2,1,0:T(8,128)(2,1)} %slice.232.refs_1_, bf16[8,64,896]{2,1,0:T(8,128)(2,1)} %collective-permute-done.12.refs_2_, bf16[8,64,896]{2,1,0:T(8,128)(2,1)} %collective-permute-done.13.refs_3_), custom_call_target="tpu_custom_call" | custom-call | flops 469762048 | bytes 2818048 | tf_op jit(solution)/shard_map/pallas_call | solution.py:207
  121.6 3.1 %fusion.17 = f32[512,896]{1,0:T(8,128)} fusion(bf16[384,1792]{1,0:T(8,128)(2,1)} %get-tuple-element.13, pred[512,512]{1,0:T(32,128)(4,1)S(1)} %iota_compare_fusion.2), kind=kOutput, calls=%fused_computation.40 | convolution fusion | flops 352321536 | bytes 2719744 | tf_op jit(solution)/shard_map/dot_general | solution.py:18
  129.7 3.1 %fusion.11 = f32[512,896]{1,0:T(8,128)} fusion(bf16[384,1792]{1,0:T(8,128)(2,1)} %collective-permute-done.11, pred[512,512]{1,0:T(32,128)(4,1)S(1)} %iota_compare_fusion.1), kind=kOutput, calls=%fused_computation.34 | convolution fusion | flops 352321536 | bytes 2719744 | tf_op jit(solution)/shard_map/dot_general | solution.py:18
  132.8 3.0 %fusion.13 = f32[512,896]{1,0:T(8,128)} fusion(bf16[384,1792]{1,0:T(8,128)(2,1)} %collective-permute-done.11, pred[512,512]{1,0:T(32,128)(4,1)S(1)} %iota_compare_fusion.1), kind=kOutput, calls=%fused_computation.36 | convolution fusion | flops 352321536 | bytes 2719744 | tf_op jit(solution)/shard_map/dot_general | solution.py:18
  135.8 9.2 %base.3 = f32[512,896]{1,0:T(8,128)} custom-call(bf16[16,512,256]{2,1,0:T(8,128)(2,1)} %all-to-all-done.tokens_ref, bf16[4096,896]{1,0:T(8,128)(2,1)} %w_ref.4), custom_call_target="tpu_custom_call" | custom-call | flops 3758096384 | bytes 10092544 | tf_op jit(solution)/shard_map/base/pallas_call | solution.py:80
  145.0 9.2 %base.2 = f32[512,896]{1,0:T(8,128)} custom-call(bf16[16,512,256]{2,1,0:T(8,128)(2,1)} %all-to-all-done.tokens_ref, bf16[4096,896]{1,0:T(8,128)(2,1)} %w_ref.3), custom_call_target="tpu_custom_call" | custom-call | flops 3758096384 | bytes 10092544 | tf_op jit(solution)/shard_map/base/pallas_call | solution.py:80
  154.2 7.2 %multiply_convert_fusion.hidden_ref = bf16[512,896]{1,0:T(8,128)(2,1)} fusion(f32[512,896]{1,0:T(8,128)} %fusion.29, f32[512,896]{1,0:T(8,128)} %base.3, f32[512,896]{1,0:T(8,128)S(1)} %fusion.15, f32[512,896]{1,0:T(8,128)} %fusion.11, f32[512,896]{1,0:T(8,128)} %fusion.34, f32[512,896]{1,0:T(8,128)} %fusion.31, f32[512,896]{1,0:T(8,128)} %base.2, ...), kind=kOutput, calls=%fused_computation.3 | convolution fusion | flops 123863040 | bytes 17727488 | tf_op jit(solution)/shard_map/dot_general | solution.py:18
  161.5 8.6 %partial.1 = bf16[16,512,256]{2,1,0:T(8,128)(2,1)} custom-call(bf16[512,896]{1,0:T(8,128)(2,1)} %multiply_convert_fusion.hidden_ref, bf16[896,4096]{1,0:T(8,128)(2,1)} %w_ref.5), custom_call_target="tpu_custom_call" | custom-call | flops 3758096384 | bytes 12451840 | tf_op jit(solution)/shard_map/partial/pallas_call | solution.py:108
  170.1 6.8 %all-to-all-start.3 = ((bf16[16,512,256]{2,1,0:T(8,128)(2,1)}), bf16[16,512,256]{2,1,0:T(8,128)(2,1)}, u32[]{:S(2)}, u32[]{:S(2)}) async-start(bf16[16,512,256]{2,1,0:T(8,128)(2,1)} %partial.1), calls=%async_computation.3 | async-start | bytes 8388608 | tf_op jit(solution)/shard_map/all_to_all | solution.py:35
  177.6 3.0 %collective-permute-start.19 = (bf16[4,64,1152]{2,1,0:T(8,128)(2,1)S(1)}, bf16[4,64,1152]{2,1,0:T(8,128)(2,1)S(1)}, u32[]{:S(2)}, u32[]{:S(2)}) collective-permute-start(bf16[4,64,1152]{2,1,0:T(8,128)(2,1)S(1)} %pad_maximum_fusion.2.refs_3_), channel_id=1, source_target_pairs={{0,96},{32,0},{64,32},{96,64},{1,97},{33,1},{65,33},{97,65},{2,98}... | collective-permute-start | bytes 1769480 | tf_op jit(solution)/shard_map/ppermute | solution.py:27
  180.7 3.2 %collective-permute-start.18 = (bf16[4,64,1152]{2,1,0:T(8,128)(2,1)S(1)}, bf16[4,64,1152]{2,1,0:T(8,128)(2,1)S(1)}, u32[]{:S(2)}, u32[]{:S(2)}) collective-permute-start(bf16[4,64,1152]{2,1,0:T(8,128)(2,1)S(1)} %pad_maximum_fusion.1.refs_2_), channel_id=1, source_target_pairs={{0,96},{32,0},{64,32},{96,64},{1,97},{33,1},{65,33},{97,65},{2,98}... | collective-permute-start | bytes 1769480 | tf_op jit(solution)/shard_map/ppermute | solution.py:27
  183.9 10.8 %collective-permute-done.16.refs_4_ = bf16[4,64,1152]{2,1,0:T(8,128)(2,1)S(1)} collective-permute-done((bf16[4,64,1152]{2,1,0:T(8,128)(2,1)S(1)}, bf16[4,64,1152]{2,1,0:T(8,128)(2,1)S(1)}, u32[]{:S(2)}, u32[]{:S(2)}) %collective-permute-start.16) | collective-permute-done | bytes 589856 | tf_op jit(solution)/shard_map/ppermute | solution.py:27
  194.7 3.4 %collective-permute-start.21 = (bf16[4,64,1152]{2,1,0:T(8,128)(2,1)S(1)}, bf16[4,64,1152]{2,1,0:T(8,128)(2,1)}, u32[]{:S(2)}, u32[]{:S(2)}) collective-permute-start(bf16[4,64,1152]{2,1,0:T(8,128)(2,1)S(1)} %collective-permute-done.19.refs_7_), channel_id=1, source_target_pairs={{0,96},{32,0},{64,32},{96,64},{1,97},{33,1},{65,33},{97,65},{2,98}... | collective-permute-start | bytes 1769480 | tf_op jit(solution)/shard_map/ppermute | solution.py:27
  201.0 6.4 %collective-permute-done.17.refs_5_ = bf16[4,64,1152]{2,1,0:T(8,128)(2,1)S(1)} collective-permute-done((bf16[4,64,1152]{2,1,0:T(8,128)(2,1)S(1)}, bf16[4,64,1152]{2,1,0:T(8,128)(2,1)S(1)}, u32[]{:S(2)}, u32[]{:S(2)}) %collective-permute-start.17) | collective-permute-done | bytes 589856 | tf_op jit(solution)/shard_map/ppermute | solution.py:27
  207.4 11.9 %collective-permute-done.20.refs_8_ = bf16[4,64,1152]{2,1,0:T(8,128)(2,1)S(1)} collective-permute-done((bf16[4,64,1152]{2,1,0:T(8,128)(2,1)S(1)}, bf16[4,64,1152]{2,1,0:T(8,128)(2,1)S(1)}, u32[]{:S(2)}, u32[]{:S(2)}) %collective-permute-start.20) | collective-permute-done | bytes 589856 | tf_op jit(solution)/shard_map/ppermute | solution.py:27
  220.0 5.6 %shard_map.102 = (bf16[512,64]{1,0:T(8,128)(2,1)}, bf16[512,64]{1,0:T(8,128)(2,1)}) custom-call(bf16[4,256,896]{2,1,0:T(8,128)(2,1)} %pad_maximum_fusion.refs_0_, bf16[4,256,1]{2,1,0:T(8,128)(2,1)} %copy-done.2, bf16[4,64,1152]{2,1,0:T(8,128)(2,1)} %copy-done, bf16[4,64,1152]{2,1,0:T(8,128)(2,1)} %copy-done.1, bf16[4,64,1152]{2,1,0:T(8,128)(2,1)} %copy-done.5, ...), custom_call_target="tpu_custom_call" | custom-call | flops 939524096 | bytes 6684672 | tf_op jit(solution)/shard_map/pallas_call | solution.py:207
  229.0 3.2 %collective-permute-start.25 = (bf16[512,64]{0,1:T(8,128)(2,1)S(1)}, bf16[512,64]{0,1:T(8,128)(2,1)S(1)}, u32[]{:S(2)}, u32[]{:S(2)}) collective-permute-start(bf16[512,64]{0,1:T(8,128)(2,1)S(1)} %fusion.7), channel_id=1, source_target_pairs={{0,8},{4,12},{8,0},{12,4},{1,9},{5,13},{9,1},{13,5},{2,10},{6,14},... | collective-permute-start | bytes 196616 | tf_op jit(solution)/shard_map/ppermute | solution.py:27
  234.2 2.8 %collective-permute-done.25 = bf16[512,64]{0,1:T(8,128)(2,1)S(1)} collective-permute-done((bf16[512,64]{0,1:T(8,128)(2,1)S(1)}, bf16[512,64]{0,1:T(8,128)(2,1)S(1)}, u32[]{:S(2)}, u32[]{:S(2)}) %collective-permute-start.25) | collective-permute-done | bytes 65568 | tf_op jit(solution)/shard_map/ppermute | solution.py:27
  238.8 3.0 %collective-permute-start.28 = (bf16[512,64]{0,1:T(8,128)(2,1)S(1)}, bf16[512,64]{0,1:T(8,128)(2,1)S(1)}, u32[]{:S(2)}, u32[]{:S(2)}) collective-permute-start(bf16[512,64]{0,1:T(8,128)(2,1)S(1)} %add_convert_fusion.1), channel_id=1, source_target_pairs={{0,2},{1,3},{2,0},{3,1},{4,6},{5,7},{6,4},{7,5},{8,10},{9,11},{10,... | collective-permute-start | bytes 196616 | tf_op jit(solution)/shard_map/ppermute | solution.py:27
  251.1 4.0 %shard_map.103 = (bf16[512,256]{1,0:T(8,128)(2,1)}, bf16[512,256]{1,0:T(8,128)(2,1)}) custom-call(bf16[4,256,64]{2,1,0:T(8,128)(2,1)} %pad_maximum_fusion.3.refs_0_, bf16[4,256,1]{2,1,0:T(8,128)(2,1)} %copy-done.2, bf16[4,64,1152]{2,1,0:T(8,128)(2,1)} %copy-done, bf16[4,64,1152]{2,1,0:T(8,128)(2,1)} %copy-done.1, bf16[4,64,1152]{2,1,0:T(8,128)(2,1)} %copy-done.5, ...), custom_call_target="tpu_custom_call" | custom-call | flops 268435456 | bytes 5373952 | tf_op jit(solution)/shard_map/pallas_call | solution.py:207
  257.2 2.8 %convert_reduce_fusion = f32[512,256]{1,0:T(8,128)S(1)} fusion(bf16[16,512,256]{2,1,0:T(8,128)(2,1)} %all-to-all-done.3), kind=kLoop, calls=%fused_computation | loop fusion | flops 4063232 | bytes 4718592 | tf_op jit(solution)/shard_map/reduce_sum | solution.py:336
  (171 shorter events, 55.0 us)
Async XLA Ops:
  0.0 6.1 %collective-permute-start = (s32[512]{0:T(512)}, s32[512]{0:T(512)S(1)}, u32[]{:S(2)}, u32[]{:S(2)}) collective-permute-start(s32[512]{0:T(512)} %param.11), channel_id=1, source_target_pairs={{0,16},{16,0},{1,17},{17,1},{2,18},{18,2},{3,19},{19,3},{4,20},{20... | collective-permute-start | bytes 6152 | tf_op jit(solution)/shard_map/ppermute | solution.py:27
  0.0 29.2 %collective-permute-start.4 = (bf16[8,256,128]{2,1,0:T(8,128)(2,1)}, bf16[8,256,128]{2,1,0:T(8,128)(2,1)S(1)}, u32[]{:S(2)}, u32[]{:S(2)}) collective-permute-start(bf16[8,256,128]{2,1,0:T(8,128)(2,1)} %param.16), channel_id=1, source_target_pairs={{0,64},{32,96},{64,0},{96,32},{1,65},{33,97},{65,1},{97,33},{2,66}... | collective-permute-start | bytes 1572872 | tf_op jit(solution)/shard_map/ppermute | solution.py:27
  4.1 24.7 %collective-permute-start.3 = (bf16[8,256,128]{2,1,0:T(8,128)(2,1)}, bf16[8,256,128]{2,1,0:T(8,128)(2,1)S(1)}, u32[]{:S(2)}, u32[]{:S(2)}) collective-permute-start(bf16[8,256,128]{2,1,0:T(8,128)(2,1)} %param.16), channel_id=1, source_target_pairs={{0,96},{32,0},{64,32},{96,64},{1,97},{33,1},{65,33},{97,65},{2,98}... | collective-permute-start | bytes 1572872 | tf_op jit(solution)/shard_map/ppermute | solution.py:27
  4.8 24.8 %collective-permute-start.2 = (bf16[8,256,128]{2,1,0:T(8,128)(2,1)}, bf16[8,256,128]{2,1,0:T(8,128)(2,1)S(1)}, u32[]{:S(2)}, u32[]{:S(2)}) collective-permute-start(bf16[8,256,128]{2,1,0:T(8,128)(2,1)} %param.16), channel_id=1, source_target_pairs={{0,32},{32,64},{64,96},{96,0},{1,33},{33,65},{65,97},{97,1},{2,34}... | collective-permute-start | bytes 1572872 | tf_op jit(solution)/shard_map/ppermute | solution.py:27
  6.1 5.6 %collective-permute-start.1 = (bf16[512,256]{1,0:T(8,128)(2,1)}, bf16[512,256]{1,0:T(8,128)(2,1)S(1)}, u32[]{:S(2)}, u32[]{:S(2)}) collective-permute-start(bf16[512,256]{1,0:T(8,128)(2,1)} %param.10), channel_id=1, source_target_pairs={{0,16},{16,0},{1,17},{17,1},{2,18},{18,2},{3,19},{19,3},{4,20},{20... | collective-permute-start | bytes 786440 | tf_op jit(solution)/shard_map/ppermute | solution.py:27
  47.2 11.4 %all-to-all-start.2 = ((bf16[16,32,128]{2,1,0:T(8,128)(2,1)}), bf16[16,32,128]{2,1,0:T(8,128)(2,1)S(1)}, u32[]{:S(2)}, u32[]{:S(2)}) async-start(bf16[16,32,128]{2,1,0:T(8,128)(2,1)} %broadcast_in_dim.30), calls=%async_computation.2 | async-start | bytes 262144 | tf_op jit(solution)/shard_map/all_to_all | solution.py:35
  52.4 44.4 %collective-permute-start.10 = (bf16[8,64,896]{2,1,0:T(8,128)(2,1)S(1)}, bf16[8,64,896]{2,1,0:T(8,128)(2,1)}, u32[]{:S(2)}, u32[]{:S(2)}) collective-permute-start(bf16[8,64,896]{2,1,0:T(8,128)(2,1)S(1)} %get-tuple-element.26.refs_3_), channel_id=1, source_target_pairs={{0,96},{32,0},{64,32},{96,64},{1,97},{33,1},{65,33},{97,65},{2,98}... | collective-permute-start | bytes 2752520 | tf_op jit(solution)/shard_map/ppermute | solution.py:27
  55.1 48.3 %collective-permute-start.8 = (bf16[8,64,896]{2,1,0:T(8,128)(2,1)S(1)}, bf16[8,64,896]{2,1,0:T(8,128)(2,1)}, u32[]{:S(2)}, u32[]{:S(2)}) collective-permute-start(bf16[8,64,896]{2,1,0:T(8,128)(2,1)S(1)} %get-tuple-element.26.refs_3_), channel_id=1, source_target_pairs={{0,32},{32,64},{64,96},{96,0},{1,33},{33,65},{65,97},{97,1},{2,34}... | collective-permute-start | bytes 2752520 | tf_op jit(solution)/shard_map/ppermute | solution.py:27
  55.1 41.7 %collective-permute-start.7 = (bf16[8,64,896]{2,1,0:T(8,128)(2,1)S(1)}, bf16[8,64,896]{2,1,0:T(8,128)(2,1)}, u32[]{:S(2)}, u32[]{:S(2)}) collective-permute-start(bf16[8,64,896]{2,1,0:T(8,128)(2,1)S(1)} %get-tuple-element.27.refs_2_), channel_id=1, source_target_pairs={{0,32},{32,64},{64,96},{96,0},{1,33},{33,65},{65,97},{97,1},{2,34}... | collective-permute-start | bytes 2752520 | tf_op jit(solution)/shard_map/ppermute | solution.py:27
  55.1 48.3 %collective-permute-start.9 = (bf16[8,64,896]{2,1,0:T(8,128)(2,1)S(1)}, bf16[8,64,896]{2,1,0:T(8,128)(2,1)}, u32[]{:S(2)}, u32[]{:S(2)}) collective-permute-start(bf16[8,64,896]{2,1,0:T(8,128)(2,1)S(1)} %get-tuple-element.27.refs_2_), channel_id=1, source_target_pairs={{0,96},{32,0},{64,32},{96,64},{1,97},{33,1},{65,33},{97,65},{2,98}... | collective-permute-start | bytes 2752520 | tf_op jit(solution)/shard_map/ppermute | solution.py:27
  61.1 74.7 %all-to-all-start = ((bf16[16,512,256]{2,1,0:T(8,128)(2,1)}), bf16[16,512,256]{2,1,0:T(8,128)(2,1)}, u32[]{:S(2)}, u32[]{:S(2)}) async-start(bf16[16,512,256]{2,1,0:T(8,128)(2,1)} %broadcast_in_dim.27), calls=%async_computation | async-start | bytes 8388608 | tf_op jit(solution)/shard_map/all_to_all | solution.py:35
  72.3 29.1 %collective-permute-start.6 = (bf16[512,128]{1,0:T(8,128)(2,1)}, bf16[512,128]{1,0:T(8,128)(2,1)S(1)}, u32[]{:S(2)}, u32[]{:S(2)}) collective-permute-start(bf16[512,128]{1,0:T(8,128)(2,1)} %bitcast.101), channel_id=1, source_target_pairs={{0,16},{16,0},{1,17},{17,1},{2,18},{18,2},{3,19},{19,3},{4,20},{20... | collective-permute-start | bytes 393224 | tf_op jit(solution)/shard_map/ppermute | solution.py:27
  96.8 21.4 %collective-permute-start.12 = (bf16[8,64,896]{2,1,0:T(8,128)(2,1)}, bf16[8,64,896]{2,1,0:T(8,128)(2,1)}, u32[]{:S(2)}, u32[]{:S(2)}) collective-permute-start(bf16[8,64,896]{2,1,0:T(8,128)(2,1)} %collective-permute-done.7.refs_4_), channel_id=1, source_target_pairs={{0,32},{32,64},{64,96},{96,0},{1,33},{33,65},{65,97},{97,1},{2,34}... | collective-permute-start | bytes 2752520 | tf_op jit(solution)/shard_map/ppermute | solution.py:27
  96.8 21.4 %collective-permute-start.13 = (bf16[8,64,896]{2,1,0:T(8,128)(2,1)}, bf16[8,64,896]{2,1,0:T(8,128)(2,1)}, u32[]{:S(2)}, u32[]{:S(2)}) collective-permute-start(bf16[8,64,896]{2,1,0:T(8,128)(2,1)} %collective-permute-done.10.refs_7_), channel_id=1, source_target_pairs={{0,96},{32,0},{64,32},{96,64},{1,97},{33,1},{65,33},{97,65},{2,98}... | collective-permute-start | bytes 2752520 | tf_op jit(solution)/shard_map/ppermute | solution.py:27
  110.4 19.2 %collective-permute-start.11 = (bf16[384,1792]{1,0:T(8,128)(2,1)}, bf16[384,1792]{1,0:T(8,128)(2,1)}, u32[]{:S(2)}, u32[]{:S(2)}) collective-permute-start(bf16[384,1792]{1,0:T(8,128)(2,1)} %get-tuple-element.14), channel_id=1, source_target_pairs={{0,16},{16,0},{1,17},{17,1},{2,18},{18,2},{3,19},{19,3},{4,20},{20... | collective-permute-start | bytes 4128776 | tf_op jit(solution)/shard_map/ppermute | solution.py:27
  121.6 4.8 %collective-permute-start.14 = (bf16[128,1792]{1,0:T(8,128)(2,1)}, bf16[128,1792]{1,0:T(8,128)(2,1)S(1)}, u32[]{:S(2)}, u32[]{:S(2)}) collective-permute-start(bf16[128,1792]{1,0:T(8,128)(2,1)} %get-tuple-element.16), channel_id=1, source_target_pairs={{0,16},{16,0},{1,17},{17,1},{2,18},{18,2},{3,19},{19,3},{4,20},{20... | collective-permute-start | bytes 1376264 | tf_op jit(solution)/shard_map/ppermute | solution.py:27
  170.1 87.1 %all-to-all-start.3 = ((bf16[16,512,256]{2,1,0:T(8,128)(2,1)}), bf16[16,512,256]{2,1,0:T(8,128)(2,1)}, u32[]{:S(2)}, u32[]{:S(2)}) async-start(bf16[16,512,256]{2,1,0:T(8,128)(2,1)} %partial.1), calls=%async_computation.3 | async-start | bytes 8388608 | tf_op jit(solution)/shard_map/all_to_all | solution.py:35
  177.0 17.7 %collective-permute-start.16 = (bf16[4,64,1152]{2,1,0:T(8,128)(2,1)S(1)}, bf16[4,64,1152]{2,1,0:T(8,128)(2,1)S(1)}, u32[]{:S(2)}, u32[]{:S(2)}) collective-permute-start(bf16[4,64,1152]{2,1,0:T(8,128)(2,1)S(1)} %pad_maximum_fusion.1.refs_2_), channel_id=1, source_target_pairs={{0,32},{32,64},{64,96},{96,0},{1,33},{33,65},{65,97},{97,1},{2,34}... | collective-permute-start | bytes 1769480 | tf_op jit(solution)/shard_map/ppermute | solution.py:27
  177.3 21.5 %collective-permute-start.15 = (bf16[512,896]{1,0:T(8,128)(2,1)}, bf16[512,896]{1,0:T(8,128)(2,1)S(1)}, u32[]{:S(2)}, u32[]{:S(2)}) collective-permute-start(bf16[512,896]{1,0:T(8,128)(2,1)} %multiply_convert_fusion.hidden_ref), channel_id=1, source_target_pairs={{0,16},{16,0},{1,17},{17,1},{2,18},{18,2},{3,19},{19,3},{4,20},{20... | collective-permute-start | bytes 2752520 | tf_op jit(solution)/shard_map/ppermute | solution.py:27
  177.6 17.1 %collective-permute-start.19 = (bf16[4,64,1152]{2,1,0:T(8,128)(2,1)S(1)}, bf16[4,64,1152]{2,1,0:T(8,128)(2,1)S(1)}, u32[]{:S(2)}, u32[]{:S(2)}) collective-permute-start(bf16[4,64,1152]{2,1,0:T(8,128)(2,1)S(1)} %pad_maximum_fusion.2.refs_3_), channel_id=1, source_target_pairs={{0,96},{32,0},{64,32},{96,64},{1,97},{33,1},{65,33},{97,65},{2,98}... | collective-permute-start | bytes 1769480 | tf_op jit(solution)/shard_map/ppermute | solution.py:27
  180.7 26.7 %collective-permute-start.17 = (bf16[4,64,1152]{2,1,0:T(8,128)(2,1)S(1)}, bf16[4,64,1152]{2,1,0:T(8,128)(2,1)S(1)}, u32[]{:S(2)}, u32[]{:S(2)}) collective-permute-start(bf16[4,64,1152]{2,1,0:T(8,128)(2,1)S(1)} %pad_maximum_fusion.2.refs_3_), channel_id=1, source_target_pairs={{0,32},{32,64},{64,96},{96,0},{1,33},{33,65},{65,97},{97,1},{2,34}... | collective-permute-start | bytes 1769480 | tf_op jit(solution)/shard_map/ppermute | solution.py:27
  180.7 26.7 %collective-permute-start.18 = (bf16[4,64,1152]{2,1,0:T(8,128)(2,1)S(1)}, bf16[4,64,1152]{2,1,0:T(8,128)(2,1)S(1)}, u32[]{:S(2)}, u32[]{:S(2)}) collective-permute-start(bf16[4,64,1152]{2,1,0:T(8,128)(2,1)S(1)} %pad_maximum_fusion.1.refs_2_), channel_id=1, source_target_pairs={{0,96},{32,0},{64,32},{96,64},{1,97},{33,1},{65,33},{97,65},{2,98}... | collective-permute-start | bytes 1769480 | tf_op jit(solution)/shard_map/ppermute | solution.py:27
  194.7 24.5 %collective-permute-start.20 = (bf16[4,64,1152]{2,1,0:T(8,128)(2,1)S(1)}, bf16[4,64,1152]{2,1,0:T(8,128)(2,1)S(1)}, u32[]{:S(2)}, u32[]{:S(2)}) collective-permute-start(bf16[4,64,1152]{2,1,0:T(8,128)(2,1)S(1)} %collective-permute-done.16.refs_4_), channel_id=1, source_target_pairs={{0,32},{32,64},{64,96},{96,0},{1,33},{33,65},{65,97},{97,1},{2,34}... | collective-permute-start | bytes 1769480 | tf_op jit(solution)/shard_map/ppermute | solution.py:27
  194.7 25.3 %collective-permute-start.21 = (bf16[4,64,1152]{2,1,0:T(8,128)(2,1)S(1)}, bf16[4,64,1152]{2,1,0:T(8,128)(2,1)}, u32[]{:S(2)}, u32[]{:S(2)}) collective-permute-start(bf16[4,64,1152]{2,1,0:T(8,128)(2,1)S(1)} %collective-permute-done.19.refs_7_), channel_id=1, source_target_pairs={{0,96},{32,0},{64,32},{96,64},{1,97},{33,1},{65,33},{97,65},{2,98}... | collective-permute-start | bytes 1769480 | tf_op jit(solution)/shard_map/ppermute | solution.py:27
  225.7 1.6 collective-permute-start.22
  229.0 7.9 %collective-permute-start.25 = (bf16[512,64]{0,1:T(8,128)(2,1)S(1)}, bf16[512,64]{0,1:T(8,128)(2,1)S(1)}, u32[]{:S(2)}, u32[]{:S(2)}) collective-permute-start(bf16[512,64]{0,1:T(8,128)(2,1)S(1)} %fusion.7), channel_id=1, source_target_pairs={{0,8},{4,12},{8,0},{12,4},{1,9},{5,13},{9,1},{13,5},{2,10},{6,14},... | collective-permute-start | bytes 196616 | tf_op jit(solution)/shard_map/ppermute | solution.py:27
  232.2 4.8 %collective-permute-start.24 = (bf16[512,64]{0,1:T(8,128)(2,1)S(1)}, bf16[512,64]{0,1:T(8,128)(2,1)S(1)}, u32[]{:S(2)}, u32[]{:S(2)}) collective-permute-start(bf16[512,64]{0,1:T(8,128)(2,1)S(1)} %fusion.7), channel_id=1, source_target_pairs={{0,12},{4,0},{8,4},{12,8},{1,13},{5,1},{9,5},{13,9},{2,14},{6,2},{... | collective-permute-start | bytes 196616 | tf_op jit(solution)/shard_map/ppermute | solution.py:27
  233.3 5.5 %collective-permute-start.23 = (bf16[512,64]{0,1:T(8,128)(2,1)S(1)}, bf16[512,64]{0,1:T(8,128)(2,1)S(1)}, u32[]{:S(2)}, u32[]{:S(2)}) collective-permute-start(bf16[512,64]{0,1:T(8,128)(2,1)S(1)} %fusion.7), channel_id=1, source_target_pairs={{0,4},{4,8},{8,12},{12,0},{1,5},{5,9},{9,13},{13,1},{2,6},{6,10},{... | collective-permute-start | bytes 196616 | tf_op jit(solution)/shard_map/ppermute | solution.py:27
  238.8 6.4 %collective-permute-start.28 = (bf16[512,64]{0,1:T(8,128)(2,1)S(1)}, bf16[512,64]{0,1:T(8,128)(2,1)S(1)}, u32[]{:S(2)}, u32[]{:S(2)}) collective-permute-start(bf16[512,64]{0,1:T(8,128)(2,1)S(1)} %add_convert_fusion.1), channel_id=1, source_target_pairs={{0,2},{1,3},{2,0},{3,1},{4,6},{5,7},{6,4},{7,5},{8,10},{9,11},{10,... | collective-permute-start | bytes 196616 | tf_op jit(solution)/shard_map/ppermute | solution.py:27
  241.9 4.3 %collective-permute-start.27 = (bf16[512,64]{0,1:T(8,128)(2,1)S(1)}, bf16[512,64]{0,1:T(8,128)(2,1)S(1)}, u32[]{:S(2)}, u32[]{:S(2)}) collective-permute-start(bf16[512,64]{0,1:T(8,128)(2,1)S(1)} %add_convert_fusion.1), channel_id=1, source_target_pairs={{0,3},{1,0},{2,1},{3,2},{4,7},{5,4},{6,5},{7,6},{8,11},{9,8},{10,9... | collective-permute-start | bytes 196616 | tf_op jit(solution)/shard_map/ppermute | solution.py:27
  243.1 5.5 %collective-permute-start.26 = (bf16[512,64]{0,1:T(8,128)(2,1)S(1)}, bf16[512,64]{0,1:T(8,128)(2,1)S(1)}, u32[]{:S(2)}, u32[]{:S(2)}) collective-permute-start(bf16[512,64]{0,1:T(8,128)(2,1)S(1)} %add_convert_fusion.1), channel_id=1, source_target_pairs={{0,1},{1,2},{2,3},{3,0},{4,5},{5,6},{6,7},{7,4},{8,9},{9,10},{10,1... | collective-permute-start | bytes 196616 | tf_op jit(solution)/shard_map/ppermute | solution.py:27
  255.1 1.7 collective-permute-start.30
  (28 other events, 283.7 us)
